TPU v7x, 512 devices: a whole 4x4x16 slice. The times are simulated.
512 devices in a mesh: segment: 8 (over x, core), frames: 64 (over y, z).
Axes of the slice: x: 4, y: 4, z: 16, core: 2. Of those that a mesh axis runs over, the one named last changes fastest.
Arguments:
- hidden: bfloat16 [8, 16384, 1536], P('segment', 'frames'), may hold values from -3 to 3
- features: bfloat16 [4096, 768], P('frames'), may hold values from -160 to 160, as said below
- kv_weight: bfloat16 [8, 768, 3072], P('segment', None, 'frames'), may hold values from -0.21875 to 0.21875
- mod_table: float32 [8, 32, 3, 1536], P('segment'), may hold values from -4 to 4
- timestep: int32 [8, 256], P('segment', 'frames'), may hold values from 0 to 31
- block_list: int32 [8, 256, 4], P('segment', 'frames'), may hold values from 0 to 63
- block_count: int32 [8, 256], P('segment', 'frames'), may hold values from 1 to 4, as said below
Outputs:
- handed: bfloat16 [8, 16384, 1536], P('segment', 'frames')
Inputs may be any that keep to these rules, and one draw needn't show every extreme that they name: `features`: drawn as normal values, rows may carry common scales; within the bounds given. `block_list`: entry j of a block's list counts when j < the block's count; the others are ignored. `block_count`: the 4 frame blocks of one device have at most 10 live list entries together, and in every section some device has exactly 10.
All inputs are finite; a program needn't handle non-finite values.
Results may differ from a plain program's by a relative error of at most 0.0044.
The roundings to bfloat16 on the way count: a program that leaves them out, or rounds other values in their place, can miss the bound.
Values may be sent and summed in bfloat16 or wider, within the bound.
No kernel may reach another device: no remote copies, remote signals or barrier semaphores. Data moves between devices by JAX's collectives and lax.ppermute only.
A program may use at most 64 MiB of HBM per device.

v0:
```python
import jax
import jax.numpy as jnp
from jax import lax
from jax.sharding import PartitionSpec as P

HEADS = 12
HD = 128
BLK = 64


def from_behind(block, axis, distance):
    devices = range(lax.axis_size(axis))
    route = [((i - distance) % len(devices), i) for i in devices]
    return lax.ppermute(block, axis, route)


def local(hidden, features, kv_weight, mod_table, timestep, block_list, block_count):
    feature_table = lax.all_gather(features, "frames", axis=0, tiled=True)
    stream = hidden[0].astype(jnp.float32)
    tok_rows = stream.shape[0]
    feature_width = stream.shape[1]
    blocks_here = tok_rows // BLK
    normed = stream * lax.rsqrt(jnp.mean(stream * stream, axis=-1, keepdims=True) + 1e-06)
    levels = mod_table.shape[1]
    onehot = (timestep[0][:, None] == jnp.arange(levels, dtype=jnp.int32)[None, :]).astype(
        jnp.float32
    )
    modulate = jnp.sum(onehot[:, :, None, None] * mod_table[0][None], axis=1)
    normed_blocks = normed.reshape(blocks_here, BLK, feature_width)
    queries = (
        normed_blocks * (1.0 + modulate[:, 1][:, None, :]) + modulate[:, 0][:, None, :]
    ).astype(jnp.bfloat16)
    queries = queries.reshape(blocks_here, BLK, HEADS, HD)
    list_counts = block_count[0]
    list_blocks = block_list[0]
    slot_count = list_blocks.shape[1]
    offsets = jnp.arange(BLK, dtype=jnp.int32)
    inv_root = 1.0 / HD**0.5
    row_index = (list_blocks[:, :, None] * BLK + offsets[None, None, :]).reshape(-1)
    key_mask = jnp.repeat(
        jnp.arange(slot_count, dtype=jnp.int32)[None, :] < list_counts[:, None], BLK, axis=1
    )
    selected = jnp.take(feature_table, row_index, axis=0)
    key_values = jnp.dot(
        selected,
        lax.all_gather(kv_weight[0], "frames", axis=1, tiled=True),
        preferred_element_type=jnp.float32,
    ).astype(jnp.bfloat16)
    key_heads = key_values[:, :feature_width].reshape(-1, HEADS, HD)
    value_heads = key_values[:, feature_width:].reshape(-1, HEADS, HD)
    keys_part = key_heads.reshape(blocks_here, -1, HEADS, HD)
    values_part = value_heads.reshape(blocks_here, -1, HEADS, HD)
    scores = jnp.einsum("bqhd,bkhd->bhqk", queries, keys_part, preferred_element_type=jnp.float32)
    softmax_scores = scores
    softmax_scores = jnp.where(
        key_mask[:, None, None, :], softmax_scores * inv_root, jnp.float32(-1e30)
    )
    top_score = jnp.max(softmax_scores, axis=-1, keepdims=True)
    expo = jnp.exp(softmax_scores - top_score)
    weights = (expo / jnp.sum(expo, axis=-1, keepdims=True)).astype(jnp.bfloat16)
    mixed_heads = jnp.einsum(
        "bhqk,bkhd->bqhd", weights, values_part, preferred_element_type=jnp.float32
    )
    part_blocks = blocks_here - 0
    mixed_rows = mixed_heads.reshape(part_blocks * BLK, feature_width)
    gate_rows = jnp.repeat(modulate[0:blocks_here, 2], BLK, axis=0)
    result = (stream + gate_rows * mixed_rows).astype(jnp.bfloat16)
    handed = from_behind(result[None], "segment", 1)
    return handed


def solution(mesh):
    placed = (
        P("segment", "frames", None),
        P("frames", None),
        P("segment", None, "frames"),
        P("segment", None, None, None),
        P("segment", "frames"),
        P("segment", "frames", None),
        P("segment", "frames"),
    )
    return jax.shard_map(
        local, mesh=mesh, in_specs=placed, out_specs=P("segment", "frames", None), check_vma=False
    )
```

profile of v0, /device:TPU:32, one launch (start us, length us, event | category | flops | bytes accessed | tf_op | source)
XLA Modules:
  0.0 365.3 jit_solution(4835332354557125818)
XLA Ops:
  6.5 0.7 all-gather.4.cloned.1.call-update
  7.3 0.7 all-gather.6.cloned.1.call-update
  8.0 0.7 multiply_bitcast_fusion
  8.7 0.1 iota_add_fusion
  8.8 0.1 add.89
  8.9 0.1 add.86
  8.9 1.6 reshape.134
  10.5 0.7 fusion.21
  11.2 0.4 multiply_reduce_fusion
  11.6 0.2 fusion.20
  11.8 0.2 multiply_reduce_fusion.1
  12.1 0.1 rsqrt.12
  12.2 0.1 broadcast_in_dim.41
  12.3 0.1 broadcast_in_dim.42
  12.4 1.4 add_convert_fusion
  13.8 152.8 %all-gather.4.cloned.1.call-done = bf16[4096,768]{1,0:T(8,128)(2,1)} async-done(((bf16[64,768]{1,0:T(8,128)(2,1)}), bf16[4096,768]{1,0:T(8,128)(2,1)}) %all-gather.4.cloned.1.call-update) | async-done | bytes 6291472 | tf_op jit(solution)/shard_map/all_gather | solution.py:18
  166.6 8.1 %gather_fusion = bf16[1024,768]{1,0:T(8,128)(2,1)S(1)} fusion(bf16[4096,768]{1,0:T(8,128)(2,1)} %all-gather.4.cloned.1.call-done, s32[1024]{0:T(1024)S(1)} %broadcast_clamp_fusion), kind=kCustom, calls=%fused_computation | custom fusion | bytes 3149824 | tf_op jit(solution)/shard_map/jit(_take)/gather | solution.py:43
  174.7 137.1 %all-gather.6.cloned.1.call-done = bf16[1,768,3072]{1,2,0:T(8,128)(2,1)} async-done(((bf16[1,768,48]{1,2,0:T(8,128)(2,1)}), bf16[1,768,3072]{1,2,0:T(8,128)(2,1)}) %all-gather.6.cloned.1.call-update) | async-done | bytes 4718608 | tf_op jit(solution)/shard_map/all_gather | solution.py:46
  311.8 7.9 %convolution_convert_fusion = bf16[1024,3072]{1,0:T(8,128)(2,1)S(1)} fusion(bf16[1,768,3072]{1,2,0:T(8,128)(2,1)} %all-gather.6.cloned.1.call-done, bf16[1024,768]{1,0:T(8,128)(2,1)S(1)} %gather_fusion, pred[1024]{0:T(1024)(128)(4,1)S(1)} %compare_and_fusion), kind=kOutput, calls=%fused_computation.2 | convolution fusion | flops 4835770368 | bytes 12583936 | tf_op jit(solution)/shard_map/dot_general | solution.py:44
  319.6 2.2 fusion.25
  321.8 6.9 %reshape.144 = bf16[4,256,12,128]{3,2,1,0:T(8,128)(2,1)} reshape(bf16[1024,1536]{1,0:T(8,128)(2,1)} %get-tuple-element.8) | data formatting | bytes 6291456 | tf_op jit(solution)/shard_map/reshape;reshape | solution.py:52
  328.7 3.6 reshape.145
  332.3 3.7 %fusion.2 = f32[4,12,64,256]{3,2,1,0:T(8,128)S(1)} fusion(bf16[4,256,12,128]{3,2,1,0:T(8,128)(2,1)} %reshape.145, bf16[4,64,12,128]{3,2,1,0:T(8,128)(2,1)} %add_convert_fusion), kind=kOutput, calls=%fused_computation.4 | convolution fusion | flops 201326592 | bytes 7077888 | tf_op jit(solution)/shard_map/bqhd,bkhd->bhqk/dot_general | solution.py:53
  336.1 1.4 fusion.26
  337.5 0.8 copy-done.2
  338.2 2.4 fusion.15
  340.7 0.9 copy.24
  341.6 1.4 reshape.133
  343.0 0.2 broadcast_in_dim.38
  343.2 1.8 fusion.8
  345.0 12.6 %collective-permute-done = bf16[1,256,1536]{2,1,0:T(8,128)(2,1)S(1)} collective-permute-done((bf16[1,256,1536]{2,1,0:T(8,128)(2,1)S(1)}, bf16[1,256,1536]{2,1,0:T(8,128)(2,1)S(1)}, u32[]{:S(2)}, u32[]{:S(2)}) %collective-permute-start) | collective-permute-done | bytes 786464 | tf_op jit(solution)/shard_map/ppermute | solution.py:14
  357.6 0.9 copy.41
  (20 shorter events, 0.2 us)
Async XLA Ops:
  6.5 5.3 %copy-start = (bf16[1,256,1536]{2,1,0:T(8,128)(2,1)S(1)}, bf16[1,256,1536]{2,1,0:T(8,128)(2,1)}, u32[]{:S(2)}) copy-start(bf16[1,256,1536]{2,1,0:T(8,128)(2,1)} %param.7) | copy-start | bytes 2359300
  6.5 4.7 %copy-start.3 = (f32[1,32,3,1536]{3,1,2,0:T(8,128)S(1)}, f32[1,32,3,1536]{3,1,2,0:T(8,128)}, u32[]{:S(2)}) copy-start(f32[1,32,3,1536]{3,1,2,0:T(8,128)} %param.10) | copy-start | bytes 1769476
  6.5 5.6 %copy-start.4 = (s32[1,4]{1,0:T(1,128)S(1)}, s32[1,4]{1,0:T(1,128)}, u32[]{:S(2)}) copy-start(s32[1,4]{1,0:T(1,128)} %param.13) | copy-start | bytes 52
  6.5 160.1 %all-gather.4.cloned.1.call-start = ((), (), s32[]{:S(2)}) async-start(), calls=%async_computation | async-start | bytes 6389760 | tf_op jit(solution)/shard_map/all_gather | solution.py:18
  7.3 304.5 %all-gather.6.cloned.1.call-start = ((), (), s32[]{:S(2)}) async-start(), calls=%async_computation.1 | async-start | bytes 4792320 | tf_op jit(solution)/shard_map/all_gather | solution.py:46
  336.0 2.2 copy-start.2
  341.6 1.6 copy-start.1
  345.0 12.6 %collective-permute-start = (bf16[1,256,1536]{2,1,0:T(8,128)(2,1)S(1)}, bf16[1,256,1536]{2,1,0:T(8,128)(2,1)S(1)}, u32[]{:S(2)}, u32[]{:S(2)}) collective-permute-start(bf16[1,256,1536]{2,1,0:T(8,128)(2,1)S(1)} %fusion.8), channel_id=1, source_target_pairs={{448,0},{0,64},{64,128},{128,192},{192,256},{256,320},{320,384},{3... | collective-permute-start | bytes 2359304 | tf_op jit(solution)/shard_map/ppermute | solution.py:14
Sparse Core Ops, SparseCore 0:
  10.3 156.2 all-gather.3
  169.6 142.1 all-gather.5
where the time goes:
time: 366 us; the launch traced here: 365 us
  waiting for transfers between devices  304 us (83%)
  local copies, waits for them, and re-layouts  26.9 us (7%)
  matrix products  14 us (4%)
  between operations  13.6 us (4%)
  other arithmetic  6.91 us (2%)
    all_gather x1, waiting for transfers between devices, local(): feature_table = lax.all_gather(features, 'frames', axis=0, tiled=True)  153 us
    all_gather x1, waiting for transfers between devices, local(): lax.all_gather(kv_weight[0], 'frames', axis=1, tiled=True)  137 us
    ppermute x1, waiting for transfers between devices, from_behind(): return lax.ppermute(block, axis, route)  12.6 us
    gather x1, local copies, waits for them, and re-layouts, local(): selected = jnp.take(feature_table, row_index, axis=0)  8.07 us
    dot_general x1, matrix products, local(): jnp.dot(selected, lax.all_gather(kv_weight[0], 'frames', axis=1, tiled=Tr...  7.88 us
  transfers between devices with their start and end apart: 3, of which 3 were waited for; matrix products, arithmetic and copies ran while one was open for 4% of the time, Pallas kernels for 0%

commit v1 on v0

v1 whole, which is shorter than its diff:
```python
import jax
import jax.numpy as jnp
from jax import lax
from jax.experimental import pallas as pl
from jax.experimental.pallas import tpu as pltpu
from jax.sharding import PartitionSpec as P

HEADS = 12
HD = 128
BLK = 64
DW = 1536
FW = 768
SEL = 4
LIVE = 10
Y = 4
Z = 16
SEG = 8
PART = BLK // SEG
COLS = 48
HALF = DW // 2
Y_GROUPS = [[y * Z + z for y in range(Y)] for z in range(Z)]
Z_GROUPS = [[y * Z + z for z in range(Z)] for y in range(Y)]


def from_behind(block, axis, distance):
    devices = range(lax.axis_size(axis))
    route = [((i - distance) % len(devices), i) for i in devices]
    return lax.ppermute(block, axis, route)


def attend(first, start, count, x_ref, q_ref, hid_ref, gate_ref, w_ref, out_ref, wv, kv, sem):
    copies = []
    for i, part in enumerate((0, 2, 1, 3)):
        copy = pltpu.make_async_copy(w_ref.at[:, part], wv.at[part], sem.at[i])
        copy.start()
        copies.append(copy)
    inv_root = 1.0 / HD**0.5
    slot = lax.broadcasted_iota(jnp.int32, (BLK, SEL * BLK), 1) // BLK
    for half in range(2):
        for i, part in ((2 * half, half), (2 * half + 1, half + 2)):
            copies[i].wait()
            w = wv[part].reshape(Z * COLS, FW)
            kv[part] = lax.dot_general(
                x_ref[...], w, (((1,), (1,)), ((), ())), preferred_element_type=jnp.float32
            ).astype(jnp.bfloat16)
        for b in range(4):
            rows = slice(b * BLK, (b + 1) * BLK)
            window = pl.ds(pl.multiple_of(first[b] * BLK, BLK), SEL * BLK)
            here = slot + first[b]
            mask = (here >= start[b]) & (here < start[b] + count[b])
            for h in range(HEADS // 2):
                inner = slice(h * HD, (h + 1) * HD)
                cols = slice(half * HALF + h * HD, half * HALF + (h + 1) * HD)
                scores = lax.dot_general(
                    q_ref[rows, cols],
                    kv[half, window, inner],
                    (((1,), (1,)), ((), ())),
                    preferred_element_type=jnp.float32,
                )
                scores = jnp.where(mask, scores * inv_root, jnp.float32(-1e30))
                top = jnp.max(scores, axis=-1, keepdims=True)
                expo = jnp.exp(scores - top)
                weights = (expo / jnp.sum(expo, axis=-1, keepdims=True)).astype(jnp.bfloat16)
                mixed = jnp.dot(weights, kv[half + 2, window, inner], preferred_element_type=jnp.float32)
                out_ref[rows, cols] = (
                    hid_ref[rows, cols].astype(jnp.float32) + gate_ref[b : b + 1, cols] * mixed
                ).astype(jnp.bfloat16)


def attention(first, start, count, x, q, hidden, gate, w):
    whole = lambda: pl.BlockSpec(memory_space=pltpu.VMEM)
    return pl.pallas_call(
        attend,
        out_shape=jax.ShapeDtypeStruct((4 * BLK, DW), jnp.bfloat16),
        in_specs=[pl.BlockSpec(memory_space=pltpu.SMEM)] * 3
        + [whole(), whole(), whole(), whole(), pl.BlockSpec(memory_space=pltpu.HBM)],
        out_specs=whole(),
        scratch_shapes=[
            pltpu.VMEM((Y, Z, COLS, FW), jnp.bfloat16),
            pltpu.VMEM((Y, LIVE * BLK, HALF), jnp.bfloat16),
            pltpu.SemaphoreType.DMA((4,)),
        ],
        compiler_params=pltpu.CompilerParams(vmem_limit_bytes=40 * 1024 * 1024),
    )(first, start, count, x, q, hidden, gate, w)


def copy_rows(spot, table_ref, out_ref):
    for n in range(SEG * LIVE):
        out_ref[n] = table_ref[spot[n]]


def pick(spot, table):
    whole = pl.BlockSpec(memory_space=pltpu.VMEM)
    return pl.pallas_call(
        copy_rows,
        out_shape=jax.ShapeDtypeStruct((SEG * LIVE, PART, FW), jnp.bfloat16),
        in_specs=[pl.BlockSpec(memory_space=pltpu.SMEM), whole],
        out_specs=whole,
    )(spot, table)


def local(hidden, features, kv_weight, mod_table, timestep, block_list, block_count):
    slab = kv_weight[0].T
    slab = lax.all_gather(slab, "frames", axis=0, tiled=True, axis_index_groups=Y_GROUPS)
    features, slab, block_list = lax.optimization_barrier((features, slab, block_list))
    weight = lax.all_gather(slab, "frames", axis=0, tiled=True, axis_index_groups=Z_GROUPS)

    counts = block_count[0]
    before = jnp.arange(4, dtype=jnp.int32)[:, None] > jnp.arange(4, dtype=jnp.int32)[None, :]
    start = jnp.sum(jnp.where(before, counts[None, :], 0), axis=1)
    entry = jnp.arange(SEL, dtype=jnp.int32)[None, :]
    place = jnp.where(entry < counts[:, None], start[:, None] + entry, -1)
    hit = place[None] == jnp.arange(LIVE, dtype=jnp.int32)[:, None, None]
    wanted = jnp.sum(jnp.where(hit, block_list[0][None], 0), axis=(1, 2))
    wanted = lax.all_gather(wanted[None], "segment", axis=0, tiled=True)

    part = lax.dynamic_slice(features, (lax.axis_index("segment") * PART, 0), (PART, FW))
    table = lax.all_gather(part, "frames", axis=0, tiled=True, axis_index_groups=Y_GROUPS)
    table = lax.all_gather(table, "frames", axis=0, tiled=True, axis_index_groups=Z_GROUPS)
    table = table.reshape(Z * Y, PART, FW)
    spot = (wanted % Z) * Y + wanted // Z
    picked = pick(spot.reshape(-1), table)
    picked = lax.all_to_all(picked.reshape(SEG, LIVE * PART, FW), "segment", 0, 0)
    picked = picked.reshape(SEG, LIVE, PART, FW).transpose(1, 0, 2, 3).reshape(LIVE * BLK, FW)

    stream = hidden[0].astype(jnp.float32)
    normed = stream * lax.rsqrt(jnp.mean(stream * stream, axis=-1, keepdims=True) + 1e-06)
    levels = mod_table.shape[1]
    onehot = (timestep[0][:, None] == jnp.arange(levels, dtype=jnp.int32)[None, :]).astype(jnp.float32)
    modulate = jnp.sum(onehot[:, :, None, None] * mod_table[0][None], axis=1)
    queries = (
        normed.reshape(4, BLK, DW) * (1.0 + modulate[:, 1][:, None, :]) + modulate[:, 0][:, None, :]
    ).astype(jnp.bfloat16)

    first = jnp.minimum(start, LIVE - SEL)
    result = attention(
        first,
        start,
        counts,
        picked,
        queries.reshape(4 * BLK, DW),
        hidden[0],
        modulate[:, 2],
        weight.reshape(Z, Y, COLS, FW),
    )
    return from_behind(result[None], "segment", 1)


def solution(mesh):
    placed = (
        P("segment", "frames", None),
        P("frames", None),
        P("segment", None, "frames"),
        P("segment", None, None, None),
        P("segment", "frames"),
        P("segment", "frames", None),
        P("segment", "frames"),
    )
    return jax.shard_map(
        local, mesh=mesh, in_specs=placed, out_specs=P("segment", "frames", None), check_vma=False
    )
```

time: 366 us -> 163 us (0.45)
  the two profiles are of different devices: /device:TPU:32 before, /device:TPU:8 now
where the time goes in v1:
time: 163 us; the launch traced here: 162 us
  blocking collectives  83.5 us (51%)
  waiting for transfers between devices  26.7 us (16%)
  Pallas kernels  23.2 us (14%)
  between operations  14.2 us (9%)
  local copies, waits for them, and re-layouts  7.72 us (5%)
  starting transfers between devices  3.7 us (2%)
  other arithmetic  3.33 us (2%)
    all_gather x1, blocking collectives, local(): lax.all_gather(table, 'frames', axis=0, tiled=True, axis_index_groups=Z_G...  48.2 us
    pallas_call x1, Pallas kernels, attention(): pl.pallas_call(attend, out_shape=jax.ShapeDtypeStruct((4 * BLK, DW), jnp....  20.9 us
    all_gather x1, blocking collectives, local(): lax.all_gather(slab, 'frames', axis=0, tiled=True, axis_index_groups=Y_GR...  17.6 us
    all_to_all x1, waiting for transfers between devices, local(): lax.all_to_all(picked.reshape(SEG, LIVE * PART, FW), 'segment', 0, 0)  14 us
    ppermute x1, waiting for transfers between devices, from_behind(): return lax.ppermute(block, axis, route)  12.6 us
    all_gather x1, blocking collectives, local(): lax.all_gather(part, 'frames', axis=0, tiled=True, axis_index_groups=Y_GR...  11.9 us
    unnamed x1, blocking collectives  5.76 us
    unnamed x20, local copies, waits for them, and re-layouts  5.76 us
  transfers between devices with their start and end apart: 3, of which 2 were waited for; matrix products, arithmetic and copies ran while one was open for 4% of the time, Pallas kernels for 1%

profile of v1, /device:TPU:8, one launch (start us, length us, event | category | flops | bytes accessed | tf_op | source)
XLA Modules:
  0.0 162.3 jit_solution(9704704117343575498)
XLA Ops:
  6.5 0.0 copy-start
  6.5 17.6 %all_gather.15 = bf16[192,768]{1,0:T(8,128)(2,1)} all-gather(bf16[48,768]{1,0:T(8,128)(2,1)} %bitcast.42), channel_id=1, replica_groups={{0,16,32,48},{1,17,33,49},{2,18,34,50},{3,19,35,51},{4,20,36,52},{5,21,..., dimensions={0}, use_global_device_ids=true | all-gather | bytes 368640 | tf_op jit(solution)/shard_map/all_gather | solution.py:104
  24.1 0.0 all-gather.3.cloned.1.call-update
  24.2 1.3 dynamic-slice
  26.1 0.8 select_reduce_fusion.1.start
  26.9 0.7 add_select_fusion.2
  27.6 0.8 select_reduce_fusion
  28.4 0.2 dynamic-update-slice
  28.6 5.8 %all-reduce = s32[80]{0:T(128)S(1)} all-reduce(s32[80]{0:T(128)S(1)} %dynamic-update-slice), channel_id=2, replica_groups=mesh['segment'=8,'frames'=64] {'segment'}, use_global_device_ids=true, to_apply=%add | all-reduce | flops 80 | bytes 640
  34.4 0.1 reshape.108
  34.5 0.6 reshape.102.spot
  35.1 11.9 %all_gather.17 = bf16[32,768]{1,0:T(8,128)(2,1)S(1)} all-gather(bf16[8,768]{1,0:T(8,128)(2,1)S(1)} %constant_dynamic-slice_fusion), channel_id=1, replica_groups={{0,16,32,48},{1,17,33,49},{2,18,34,50},{3,19,35,51},{4,20,36,52},{5,21,..., dimensions={0}, use_global_device_ids=true | all-gather | bytes 61440 | tf_op jit(solution)/shard_map/all_gather | solution.py:118
  47.0 48.2 %all_gather.18 = bf16[512,768]{1,0:T(8,128)(2,1)} all-gather(bf16[32,768]{1,0:T(8,128)(2,1)S(1)} %all_gather.17), channel_id=1, replica_groups={{0,1,2,3,4,5,6,7,8,9,10,11,12,13,14,15},{16,17,18,19,20,21,22,23,24,25,..., dimensions={0}, use_global_device_ids=true | all-gather | bytes 835584 | tf_op jit(solution)/shard_map/all_gather | solution.py:119
  95.2 2.3 %shard_map.73 = bf16[80,8,768]{2,1,0:T(8,128)(2,1)} custom-call(s32[80]{0:T(128)} %reshape.102.spot, bf16[64,8,768]{2,1,0:T(8,128)(2,1)} %bitcast.40), custom_call_target="tpu_custom_call" | custom-call | tf_op jit(solution)/shard_map/pallas_call | solution.py:94
  97.5 3.7 %all-to-all-start = ((bf16[8,80,768]{2,1,0:T(8,128)(2,1)}), bf16[8,80,768]{2,1,0:T(8,128)(2,1)S(1)}, u32[]{:S(2)}, u32[]{:S(2)}) async-start(bf16[8,80,768]{2,1,0:T(8,128)(2,1)} %bitcast.39), calls=%async_computation | async-start | bytes 1966080 | tf_op jit(solution)/shard_map/all_to_all | solution.py:123
  101.2 0.1 fusion.10
  101.3 0.4 multiply_reduce_fusion
  101.6 0.1 fusion.11
  101.7 0.2 fusion
  102.0 0.0 copy-start.3
  102.0 0.3 fusion.3.q_ref
  102.3 14.0 %all-to-all-done = bf16[8,80,768]{2,1,0:T(8,128)(2,1)S(1)} async-done(((bf16[8,80,768]{2,1,0:T(8,128)(2,1)}), bf16[8,80,768]{2,1,0:T(8,128)(2,1)S(1)}, u32[]{:S(2)}, u32[]{:S(2)}) %all-to-all-start) | async-done | bytes 983072 | tf_op jit(solution)/shard_map/all_to_all | solution.py:123
  116.4 1.0 copy-done.4
  117.4 1.3 copy.11
  118.7 0.0 all-gather.3.cloned.1.call-done
  118.7 0.0 copy-done.3
  118.7 0.0 copy-start.2
  118.7 2.3 %copy-done.2 = bf16[3072,768]{1,0:T(8,128)(2,1)S(1)} copy-done((bf16[3072,768]{1,0:T(8,128)(2,1)S(1)}, bf16[3072,768]{1,0:T(8,128)(2,1)}, u32[]{:S(2)}) %copy-start.2) | copy-done | bytes 4718616
  121.0 20.9 %shard_map.74 = bf16[256,1536]{1,0:T(8,128)(2,1)S(1)} custom-call(s32[4]{0:T(128)S(1)} %broadcast_minimum_fusion.first, s32[4]{0:T(128)S(1)} %select_reduce_fusion.1.start, s32[4]{0:T(128)S(1)} %bitcast.37, bf16[640,768]{1,0:T(8,128)(2,1)S(1)} %bitcast.32, bf16[256,1536]{1,0:T(8,128)(2,1)S(1)} %fusion.3.q_ref, bf16[256,1536]{1,0:T(8,128)(2,1)S(1)} %bitcast.30, ...), custom_call_target="tpu_custom_call" | custom-call | tf_op jit(solution)/shard_map/pallas_call | solution.py:72
  141.9 0.0 collective-permute-start
  142.0 12.6 %collective-permute-done = bf16[1,256,1536]{2,1,0:T(8,128)(2,1)S(1)} collective-permute-done((bf16[1,256,1536]{2,1,0:T(8,128)(2,1)S(1)}, bf16[1,256,1536]{2,1,0:T(8,128)(2,1)S(1)}, u32[]{:S(2)}, u32[]{:S(2)}) %collective-permute-start) | collective-permute-done | bytes 786464 | tf_op jit(solution)/shard_map/ppermute | solution.py:28
  154.6 0.9 copy.22
  (16 shorter events, 0.1 us)
Async XLA Ops:
  6.5 28.5 %copy-start = (bf16[64,768]{1,0:T(8,128)(2,1)S(1)}, bf16[64,768]{1,0:T(8,128)(2,1)}, u32[]{:S(2)}) copy-start(bf16[64,768]{1,0:T(8,128)(2,1)} %param.8) | copy-start | bytes 294916
  6.5 112.1 %all-gather.3.cloned.1.call-start = ((), (), s32[]{:S(2)}) async-start(), calls=%async_computation.1 | async-start | bytes 5013504 | tf_op jit(solution)/shard_map/all_gather | solution.py:106
  95.2 6.0 %copy-start.6 = (s32[1,4]{1,0:T(1,128)S(1)}, s32[1,4]{1,0:T(1,128)}, u32[]{:S(2)}) copy-start(s32[1,4]{1,0:T(1,128)} %param.11) | copy-start | bytes 52
  95.2 6.1 %copy-start.5 = (f32[1,32,3,1536]{3,1,2,0:T(8,128)S(1)}, f32[1,32,3,1536]{3,1,2,0:T(8,128)}, u32[]{:S(2)}) copy-start(f32[1,32,3,1536]{3,1,2,0:T(8,128)} %param.10) | copy-start | bytes 1769476
  97.5 4.2 %copy-start.1 = (bf16[1,256,1536]{2,1,0:T(8,128)(2,1)S(1)}, bf16[1,256,1536]{2,1,0:T(8,128)(2,1)}, u32[]{:S(2)}) copy-start(bf16[1,256,1536]{2,1,0:T(8,128)(2,1)} %param.7) | copy-start | bytes 2359300
  97.5 18.9 %all-to-all-start = ((bf16[8,80,768]{2,1,0:T(8,128)(2,1)}), bf16[8,80,768]{2,1,0:T(8,128)(2,1)S(1)}, u32[]{:S(2)}, u32[]{:S(2)}) async-start(bf16[8,80,768]{2,1,0:T(8,128)(2,1)} %bitcast.39), calls=%async_computation | async-start | bytes 1966080 | tf_op jit(solution)/shard_map/all_to_all | solution.py:123
  102.0 16.7 %copy-start.3 = (s32[1,4]{1,0:T(1,128)S(1)}, s32[1,4]{1,0:T(1,128)}, u32[]{:S(2)}) copy-start(s32[1,4]{1,0:T(1,128)} %param.13) | copy-start | bytes 52
  116.4 1.0 copy-start.4
  118.7 2.3 %copy-start.2 = (bf16[3072,768]{1,0:T(8,128)(2,1)S(1)}, bf16[3072,768]{1,0:T(8,128)(2,1)}, u32[]{:S(2)}) copy-start(bf16[3072,768]{1,0:T(8,128)(2,1)} %all-gather.3.cloned.1.call-done) | copy-start | bytes 14155780
  141.9 12.6 %collective-permute-start = (bf16[1,256,1536]{2,1,0:T(8,128)(2,1)S(1)}, bf16[1,256,1536]{2,1,0:T(8,128)(2,1)S(1)}, u32[]{:S(2)}, u32[]{:S(2)}) collective-permute-start(bf16[1,256,1536]{2,1,0:T(8,128)(2,1)S(1)} %bitcast.33), channel_id=1, source_target_pairs={{448,0},{0,64},{64,128},{128,192},{192,256},{256,320},{320,384},{3... | collective-permute-start | bytes 2359304 | tf_op jit(solution)/shard_map/ppermute | solution.py:28
Sparse Core Ops, SparseCore 0:
  24.3 84.6 all-gather.2

commit v2 on v1

v2 whole, which is shorter than its diff:
```python
import jax
import jax.numpy as jnp
from jax import lax
from jax.experimental import pallas as pl
from jax.experimental.pallas import tpu as pltpu
from jax.sharding import PartitionSpec as P

HEADS = 12
HD = 128
BLK = 64
DW = 1536
FW = 768
SEL = 4
LIVE = 10
Y = 4
Z = 16
SEG = 8
PART = BLK // SEG
COLS = 48
HALF = DW // 2
Y_GROUPS = [[y * Z + z for y in range(Y)] for z in range(Z)]
Z_GROUPS = [[y * Z + z for z in range(Z)] for y in range(Y)]


def from_behind(block, axis, distance):
    devices = range(lax.axis_size(axis))
    route = [((i - distance) % len(devices), i) for i in devices]
    return lax.ppermute(block, axis, route)


def attend(first, start, count, x_ref, q_ref, hid_ref, gate_ref, w_ref, out_ref, wv, kv, sem):
    copies = []
    for i, part in enumerate((0, 2, 1, 3)):
        copy = pltpu.make_async_copy(w_ref.at[:, part], wv.at[part], sem.at[i])
        copy.start()
        copies.append(copy)
    inv_root = 1.0 / HD**0.5
    slot = lax.broadcasted_iota(jnp.int32, (BLK, SEL * BLK), 1) // BLK
    windows = [pl.ds(pl.multiple_of(first[b] * BLK, BLK), SEL * BLK) for b in range(4)]

    def heads_of(half, b):
        rows = slice(b * BLK, (b + 1) * BLK)
        for h in range(HEADS // 2):
            cols = slice(half * HALF + h * HD, half * HALF + (h + 1) * HD)
            yield rows, cols, slice(h * HD, (h + 1) * HD)

    def scores_of(half, b):
        return [
            lax.dot_general(
                q_ref[rows, cols],
                kv[half, windows[b], inner],
                (((1,), (1,)), ((), ())),
                preferred_element_type=jnp.float32,
            )
            for rows, cols, inner in heads_of(half, b)
        ]

    for half in range(2):
        for i, part in ((2 * half, half), (2 * half + 1, half + 2)):
            copies[i].wait()
            kv[part] = lax.dot_general(
                x_ref[...],
                wv[part].reshape(Z * COLS, FW),
                (((1,), (1,)), ((), ())),
                preferred_element_type=jnp.float32,
            ).astype(jnp.bfloat16)
        ahead = scores_of(half, 0)
        for b in range(4):
            scores = ahead
            if b < 3:
                ahead = scores_of(half, b + 1)
            here = slot + first[b]
            mask = (here >= start[b]) & (here < start[b] + count[b])
            weights = []
            for score in scores:
                score = jnp.where(mask, score * inv_root, jnp.float32(-1e30))
                expo = jnp.exp(score - jnp.max(score, axis=-1, keepdims=True))
                weights.append((expo / jnp.sum(expo, axis=-1, keepdims=True)).astype(jnp.bfloat16))
            for weight, (rows, cols, inner) in zip(weights, heads_of(half, b)):
                mixed = jnp.dot(
                    weight, kv[half + 2, windows[b], inner], preferred_element_type=jnp.float32
                )
                out_ref[rows, cols] = (
                    hid_ref[rows, cols].astype(jnp.float32) + gate_ref[b : b + 1, cols] * mixed
                ).astype(jnp.bfloat16)


def attention(first, start, count, x, q, hidden, gate, w):
    whole = lambda: pl.BlockSpec(memory_space=pltpu.VMEM)
    return pl.pallas_call(
        attend,
        out_shape=jax.ShapeDtypeStruct((4 * BLK, DW), jnp.bfloat16),
        in_specs=[pl.BlockSpec(memory_space=pltpu.SMEM)] * 3
        + [whole(), whole(), whole(), whole(), pl.BlockSpec(memory_space=pltpu.HBM)],
        out_specs=whole(),
        scratch_shapes=[
            pltpu.VMEM((Y, Z, COLS, FW), jnp.bfloat16),
            pltpu.VMEM((Y, LIVE * BLK, HALF), jnp.bfloat16),
            pltpu.SemaphoreType.DMA((4,)),
        ],
        compiler_params=pltpu.CompilerParams(vmem_limit_bytes=40 * 1024 * 1024),
    )(first, start, count, x, q, hidden, gate, pltpu.with_memory_space_constraint(w, pltpu.HBM))


def copy_rows(spot, table_ref, out_ref):
    for n in range(SEG * LIVE):
        out_ref[n] = table_ref[spot[n]]


def pick(spot, table):
    whole = pl.BlockSpec(memory_space=pltpu.VMEM)
    return pl.pallas_call(
        copy_rows,
        out_shape=jax.ShapeDtypeStruct((SEG * LIVE, PART, FW), jnp.bfloat16),
        in_specs=[pl.BlockSpec(memory_space=pltpu.SMEM), whole],
        out_specs=whole,
    )(spot, table)


def local(hidden, features, kv_weight, mod_table, timestep, block_list, block_count):
    me = lax.axis_index("segment")
    slab = from_behind(kv_weight[0].T, "segment", 1)
    stream_in = from_behind(hidden[0], "segment", 1)
    levels = mod_table.shape[1]
    onehot = (timestep[0][:, None] == jnp.arange(levels, dtype=jnp.int32)[None, :]).astype(jnp.float32)
    modulate = jnp.sum(onehot[:, :, None, None] * mod_table[0][None], axis=1)
    modulate = from_behind(modulate.reshape(12, DW), "segment", 1).reshape(4, 3, DW)

    counts = block_count[0]
    before = jnp.arange(4, dtype=jnp.int32)[:, None] > jnp.arange(4, dtype=jnp.int32)[None, :]
    start = jnp.sum(jnp.where(before, counts[None, :], 0), axis=1)
    entry = jnp.arange(SEL, dtype=jnp.int32)[None, :]
    place = jnp.where(entry < counts[:, None], start[:, None] + entry, -1)
    hit = place[None] == jnp.arange(LIVE, dtype=jnp.int32)[:, None, None]
    wanted = jnp.sum(jnp.where(hit, block_list[0][None], 0), axis=(1, 2))
    lists = jnp.concatenate([wanted, start, counts]).reshape(1, LIVE + 8)
    lists = lax.all_gather(lists, "segment", axis=0, tiled=True)
    lists = jnp.roll(lists, 1, axis=0)
    spot = (lists[:, :LIVE] % Z) * Y + lists[:, :LIVE] // Z
    mine = lax.dynamic_slice(lists, (me, LIVE), (1, 8))[0]

    slab, spot = lax.optimization_barrier((slab, spot))
    slab = lax.all_gather(slab, "frames", axis=0, tiled=True, axis_index_groups=Y_GROUPS)
    features, slab = lax.optimization_barrier((features, slab))
    weight = lax.all_gather(slab, "frames", axis=0, tiled=True, axis_index_groups=Z_GROUPS)

    part = lax.dynamic_slice(features, (me * PART, 0), (PART, FW))
    table = lax.all_gather(part, "frames", axis=0, tiled=True, axis_index_groups=Y_GROUPS)
    table = lax.all_gather(table, "frames", axis=0, tiled=True, axis_index_groups=Z_GROUPS)
    picked = pick(spot.reshape(-1), table.reshape(Z * Y, PART, FW))
    picked = lax.all_to_all(picked.reshape(SEG, LIVE * PART, FW), "segment", 0, 0)
    picked = picked.reshape(SEG, LIVE, PART, FW).transpose(1, 0, 2, 3).reshape(LIVE * BLK, FW)

    stream = stream_in.astype(jnp.float32)
    normed = stream * lax.rsqrt(jnp.mean(stream * stream, axis=-1, keepdims=True) + 1e-06)
    queries = (
        normed.reshape(4, BLK, DW) * (1.0 + modulate[:, 1][:, None, :]) + modulate[:, 0][:, None, :]
    ).astype(jnp.bfloat16)

    result = attention(
        jnp.minimum(mine[:4], LIVE - SEL),
        mine[:4],
        mine[4:],
        picked,
        queries.reshape(4 * BLK, DW),
        stream_in,
        modulate[:, 2],
        weight.reshape(Z, Y, COLS, FW),
    )
    return result[None]


def solution(mesh):
    placed = (
        P("segment", "frames", None),
        P("frames", None),
        P("segment", None, "frames"),
        P("segment", None, None, None),
        P("segment", "frames"),
        P("segment", "frames", None),
        P("segment", "frames"),
    )
    return jax.shard_map(
        local, mesh=mesh, in_specs=placed, out_specs=P("segment", "frames", None), check_vma=False
    )
```

time: 163 us -> 142 us (0.87)
  the two profiles are of different devices: /device:TPU:8 before, /device:TPU:1 now
where the time goes in v2:
time: 142 us; the launch traced here: 141 us
  blocking collectives  74.3 us (52%)
  starting transfers between devices  16.2 us (11%)
  between operations  14.2 us (10%)
  waiting for transfers between devices  13.7 us (10%)
  Pallas kernels  12.4 us (9%)
  other arithmetic  5.9 us (4%)
  local copies, waits for them, and re-layouts  4.52 us (3%)
    all_gather x1, blocking collectives, local(): lax.all_gather(table, 'frames', axis=0, tiled=True, axis_index_groups=Z_G...  42.8 us
    all_to_all x1, waiting for transfers between devices, local(): lax.all_to_all(picked.reshape(SEG, LIVE * PART, FW), 'segment', 0, 0)  13.7 us
    unnamed x1, blocking collectives  11.9 us
    all_to_all x1, starting transfers between devices, local(): lax.all_to_all(picked.reshape(SEG, LIVE * PART, FW), 'segment', 0, 0)  10.9 us
    pallas_call x1, Pallas kernels, attention(): pl.pallas_call(attend, out_shape=jax.ShapeDtypeStruct((4 * BLK, DW), jnp....  10.2 us
    all_gather x1, blocking collectives, local(): lax.all_gather(slab, 'frames', axis=0, tiled=True, axis_index_groups=Y_GR...  10.2 us
    all_gather x1, blocking collectives, local(): lax.all_gather(part, 'frames', axis=0, tiled=True, axis_index_groups=Y_GR...  9.55 us
    ppermute x3, starting transfers between devices, from_behind(): return lax.ppermute(block, axis, route)  5.25 us
  transfers between devices with their start and end apart: 5, of which 1 were waited for; matrix products, arithmetic and copies ran while one was open for 7% of the time, Pallas kernels for 2%

profile of v2, /device:TPU:1, one launch (start us, length us, event | category | flops | bytes accessed | tf_op | source)
XLA Modules:
  0.0 141.2 jit_solution(12710707077041634540)
XLA Ops:
  6.5 2.6 %collective-permute-start = (bf16[48,768]{1,0:T(8,128)(2,1)}, bf16[48,768]{1,0:T(8,128)(2,1)S(1)}, u32[]{:S(2)}, u32[]{:S(2)}) collective-permute-start(bf16[48,768]{1,0:T(8,128)(2,1)} %bitcast.49), channel_id=1, source_target_pairs={{448,0},{0,64},{64,128},{128,192},{192,256},{256,320},{320,384},{3... | collective-permute-start | bytes 221192 | tf_op jit(solution)/shard_map/ppermute | solution.py:28
  9.1 0.8 select_reduce_fusion.1
  9.9 0.7 add_select_fusion.2
  10.6 1.3 dynamic-slice
  12.6 0.8 select_reduce_fusion
  13.3 0.8 add_dynamic-update-slice_fusion
  14.2 11.9 %all-reduce = s32[144]{0:T(256)S(1)} all-reduce(s32[144]{0:T(256)S(1)} %add_dynamic-update-slice_fusion), channel_id=2, replica_groups=mesh['segment'=8,'frames'=64] {'segment'}, use_global_device_ids=true, to_apply=%add | all-reduce | flops 144 | bytes 1152
  26.0 0.1 slice_bitcast_fusion
  26.1 0.1 reshape.116
  26.2 0.0 collective-permute-done
  26.2 10.2 %all_gather.16 = bf16[192,768]{1,0:T(8,128)(2,1)} all-gather(bf16[48,768]{1,0:T(8,128)(2,1)S(1)} %collective-permute-done), channel_id=1, replica_groups={{0,16,32,48},{1,17,33,49},{2,18,34,50},{3,19,35,51},{4,20,36,52},{5,21,..., dimensions={0}, use_global_device_ids=true | all-gather | bytes 368640 | tf_op jit(solution)/shard_map/all_gather | solution.py:143
  36.4 0.0 all-gather.3.cloned.1.call-update
  36.4 0.7 fusion.10
  37.1 1.4 %multiply_reduce_fusion = f32[4,3,1536]{2,1,0:T(4,128)S(1)} fusion(f32[32,3,1536]{2,0,1:T(8,128)} %bitcast.42, f32[4,32]{1,0:T(4,128)S(1)} %fusion.10), kind=kLoop, calls=%fused_computation | loop fusion | flops 1161216 | bytes 664064 | tf_op jit(solution)/shard_map/reduce_sum | solution.py:126
  38.6 2.6 %collective-permute-start.2 = (f32[12,1536]{1,0:T(8,128)S(1)}, f32[12,1536]{1,0:T(8,128)S(1)}, u32[]{:S(2)}, u32[]{:S(2)}) collective-permute-start(f32[12,1536]{1,0:T(8,128)S(1)} %reshape.111), channel_id=1, source_target_pairs={{448,0},{0,64},{64,128},{128,192},{192,256},{256,320},{320,384},{3... | collective-permute-start | bytes 221192 | tf_op jit(solution)/shard_map/ppermute | solution.py:28
  41.2 0.0 collective-permute-start.1
  41.3 0.1 constant_dynamic-slice_fusion
  41.4 0.1 slice_bitcast_fusion.1
  41.4 9.5 %all_gather.17 = bf16[32,768]{1,0:T(8,128)(2,1)S(1)} all-gather(bf16[8,768]{1,0:T(8,128)(2,1)S(1)} %constant_dynamic-slice_fusion.1), channel_id=1, replica_groups={{0,16,32,48},{1,17,33,49},{2,18,34,50},{3,19,35,51},{4,20,36,52},{5,21,..., dimensions={0}, use_global_device_ids=true | all-gather | bytes 61440 | tf_op jit(solution)/shard_map/all_gather | solution.py:148
  51.0 42.8 %all_gather.18 = bf16[512,768]{1,0:T(8,128)(2,1)} all-gather(bf16[32,768]{1,0:T(8,128)(2,1)S(1)} %all_gather.17), channel_id=1, replica_groups={{0,1,2,3,4,5,6,7,8,9,10,11,12,13,14,15},{16,17,18,19,20,21,22,23,24,25,..., dimensions={0}, use_global_device_ids=true | all-gather | bytes 835584 | tf_op jit(solution)/shard_map/all_gather | solution.py:149
  93.8 0.6 reshape.106.spot
  94.4 2.2 %shard_map.73 = bf16[80,8,768]{2,1,0:T(8,128)(2,1)} custom-call(s32[80]{0:T(128)} %reshape.106.spot, bf16[64,8,768]{2,1,0:T(8,128)(2,1)} %bitcast.41), custom_call_target="tpu_custom_call" | custom-call | tf_op jit(solution)/shard_map/pallas_call | solution.py:112
  96.6 10.9 %all-to-all-start = ((bf16[8,80,768]{2,1,0:T(8,128)(2,1)}), bf16[8,80,768]{2,1,0:T(8,128)(2,1)S(1)}, u32[]{:S(2)}, u32[]{:S(2)}) async-start(bf16[8,80,768]{2,1,0:T(8,128)(2,1)} %bitcast.40), calls=%async_computation | async-start | bytes 1966080 | tf_op jit(solution)/shard_map/all_to_all | solution.py:151
  107.5 0.0 collective-permute-done.2
  107.5 0.1 fusion.11
  107.6 0.2 fusion
  107.9 0.3 fusion.3.q_ref
  108.2 13.7 %all-to-all-done = bf16[8,80,768]{2,1,0:T(8,128)(2,1)S(1)} async-done(((bf16[8,80,768]{2,1,0:T(8,128)(2,1)}), bf16[8,80,768]{2,1,0:T(8,128)(2,1)S(1)}, u32[]{:S(2)}, u32[]{:S(2)}) %all-to-all-start) | async-done | bytes 983072 | tf_op jit(solution)/shard_map/all_to_all | solution.py:151
  121.9 1.0 copy-done.1
  122.8 1.3 copy.12
  124.1 0.0 all-gather.3.cloned.1.call-done
  124.2 10.2 %shard_map.74 = bf16[256,1536]{1,0:T(8,128)(2,1)} custom-call(s32[4]{0:T(128)S(1)} %broadcast_minimum_fusion.first, s32[4]{0:T(128)S(1)} %get-tuple-element.17.start, s32[4]{0:T(128)S(1)} %get-tuple-element.16.count, bf16[640,768]{1,0:T(8,128)(2,1)S(1)} %bitcast.36, bf16[256,1536]{1,0:T(8,128)(2,1)S(1)} %fusion.3.q_ref, ...), custom_call_target="tpu_custom_call" | custom-call | tf_op jit(solution)/shard_map/pallas_call | solution.py:90
  (18 shorter events, 0.2 us)
Async XLA Ops:
  6.5 34.9 %copy-start = (bf16[64,768]{1,0:T(8,128)(2,1)S(1)}, bf16[64,768]{1,0:T(8,128)(2,1)}, u32[]{:S(2)}) copy-start(bf16[64,768]{1,0:T(8,128)(2,1)} %param.8) | copy-start | bytes 294916
  6.5 34.7 %copy-start.2 = (bf16[1,256,1536]{2,1,0:T(8,128)(2,1)S(1)}, bf16[1,256,1536]{2,1,0:T(8,128)(2,1)}, u32[]{:S(2)}) copy-start(bf16[1,256,1536]{2,1,0:T(8,128)(2,1)} %param.7) | copy-start | bytes 2359300
  6.5 117.6 %all-gather.3.cloned.1.call-start = ((), (), s32[]{:S(2)}) async-start(), calls=%async_computation.1 | async-start | bytes 5013504 | tf_op jit(solution)/shard_map/all_gather | solution.py:145
  6.5 19.7 %collective-permute-start = (bf16[48,768]{1,0:T(8,128)(2,1)}, bf16[48,768]{1,0:T(8,128)(2,1)S(1)}, u32[]{:S(2)}, u32[]{:S(2)}) collective-permute-start(bf16[48,768]{1,0:T(8,128)(2,1)} %bitcast.49), channel_id=1, source_target_pairs={{448,0},{0,64},{64,128},{128,192},{192,256},{256,320},{320,384},{3... | collective-permute-start | bytes 221192 | tf_op jit(solution)/shard_map/ppermute | solution.py:28
  38.6 68.8 %collective-permute-start.2 = (f32[12,1536]{1,0:T(8,128)S(1)}, f32[12,1536]{1,0:T(8,128)S(1)}, u32[]{:S(2)}, u32[]{:S(2)}) collective-permute-start(f32[12,1536]{1,0:T(8,128)S(1)} %reshape.111), channel_id=1, source_target_pairs={{448,0},{0,64},{64,128},{128,192},{192,256},{256,320},{320,384},{3... | collective-permute-start | bytes 221192 | tf_op jit(solution)/shard_map/ppermute | solution.py:28
  41.2 66.4 %collective-permute-start.1 = (bf16[256,1536]{1,0:T(8,128)(2,1)S(1)}, bf16[256,1536]{1,0:T(8,128)(2,1)S(1)}, u32[]{:S(2)}, u32[]{:S(2)}) collective-permute-start(bf16[256,1536]{1,0:T(8,128)(2,1)S(1)} %bitcast.48), channel_id=1, source_target_pairs={{448,0},{0,64},{64,128},{128,192},{192,256},{256,320},{320,384},{3... | collective-permute-start | bytes 2359304 | tf_op jit(solution)/shard_map/ppermute | solution.py:28
  96.6 25.3 %all-to-all-start = ((bf16[8,80,768]{2,1,0:T(8,128)(2,1)}), bf16[8,80,768]{2,1,0:T(8,128)(2,1)S(1)}, u32[]{:S(2)}, u32[]{:S(2)}) async-start(bf16[8,80,768]{2,1,0:T(8,128)(2,1)} %bitcast.40), calls=%async_computation | async-start | bytes 1966080 | tf_op jit(solution)/shard_map/all_to_all | solution.py:151
  121.9 1.0 copy-start.1
Sparse Core Ops, SparseCore 0:
  36.5 81.2 all-gather.2

commit v3 on v2

--- a/solution.py
+++ b/solution.py
@@ -120,6 +120,9 @@
 def local(hidden, features, kv_weight, mod_table, timestep, block_list, block_count):
     me = lax.axis_index("segment")
     slab = from_behind(kv_weight[0].T, "segment", 1)
+    slab = lax.all_gather(slab, "frames", axis=0, tiled=True, axis_index_groups=Y_GROUPS)
+    features, slab, block_count, mod_table, hidden = lax.optimization_barrier((features, slab, block_count, mod_table, hidden))
+    weight = lax.all_gather(slab, "frames", axis=0, tiled=True, axis_index_groups=Z_GROUPS)
     stream_in = from_behind(hidden[0], "segment", 1)
     levels = mod_table.shape[1]
     onehot = (timestep[0][:, None] == jnp.arange(levels, dtype=jnp.int32)[None, :]).astype(jnp.float32)
@@ -136,17 +139,13 @@
     lists = jnp.concatenate([wanted, start, counts]).reshape(1, LIVE + 8)
     lists = lax.all_gather(lists, "segment", axis=0, tiled=True)
     lists = jnp.roll(lists, 1, axis=0)
-    spot = (lists[:, :LIVE] % Z) * Y + lists[:, :LIVE] // Z
+    spot = lists[:, :LIVE]
     mine = lax.dynamic_slice(lists, (me, LIVE), (1, 8))[0]
 
-    slab, spot = lax.optimization_barrier((slab, spot))
-    slab = lax.all_gather(slab, "frames", axis=0, tiled=True, axis_index_groups=Y_GROUPS)
-    features, slab = lax.optimization_barrier((features, slab))
-    weight = lax.all_gather(slab, "frames", axis=0, tiled=True, axis_index_groups=Z_GROUPS)
 
     part = lax.dynamic_slice(features, (me * PART, 0), (PART, FW))
-    table = lax.all_gather(part, "frames", axis=0, tiled=True, axis_index_groups=Y_GROUPS)
-    table = lax.all_gather(table, "frames", axis=0, tiled=True, axis_index_groups=Z_GROUPS)
+    table = lax.all_to_all(jnp.broadcast_to(part[None], (Z, PART, FW)), "frames", 0, 0, axis_index_groups=Z_GROUPS)
+    table = lax.all_gather(table.reshape(Z * PART, FW), "frames", axis=0, tiled=True, axis_index_groups=Y_GROUPS)
     picked = pick(spot.reshape(-1), table.reshape(Z * Y, PART, FW))
     picked = lax.all_to_all(picked.reshape(SEG, LIVE * PART, FW), "segment", 0, 0)
     picked = picked.reshape(SEG, LIVE, PART, FW).transpose(1, 0, 2, 3).reshape(LIVE * BLK, FW)

time: 142 us -> 130 us (0.915)
  the two profiles are of different devices: /device:TPU:1 before, /device:TPU:2 now
where the time goes in v3:
time: 130 us; the launch traced here: 129 us
  blocking collectives  36.8 us (28%)
  waiting for transfers between devices  33.9 us (26%)
  starting transfers between devices  22 us (17%)
  between operations  14.2 us (11%)
  Pallas kernels  12.4 us (10%)
  local copies, waits for them, and re-layouts  5.23 us (4%)
  other arithmetic  4.81 us (4%)
    all_to_all x1, starting transfers between devices, local(): lax.all_to_all(jnp.broadcast_to(part[None], (Z, PART, FW)), 'frames', 0,...  15.2 us
    all_gather x1, blocking collectives, local(): lax.all_gather(table.reshape(Z * PART, FW), 'frames', axis=0, tiled=True,...  14.9 us
    all_gather x1, waiting for transfers between devices, local(): lax.all_gather(slab, 'frames', axis=0, tiled=True, axis_index_groups=Z_GR...  13.8 us
    all_gather x1, blocking collectives, local(): lax.all_gather(slab, 'frames', axis=0, tiled=True, axis_index_groups=Y_GR...  13.6 us
    all_to_all x1, waiting for transfers between devices, local(): lax.all_to_all(picked.reshape(SEG, LIVE * PART, FW), 'segment', 0, 0)  13.2 us
    pallas_call x1, Pallas kernels, attention(): pl.pallas_call(attend, out_shape=jax.ShapeDtypeStruct((4 * BLK, DW), jnp....  10.2 us
    unnamed x1, blocking collectives  8.31 us
    ppermute x3, waiting for transfers between devices, from_behind(): return lax.ppermute(block, axis, route)  6.14 us
  transfers between devices with their start and end apart: 6, of which 5 were waited for; matrix products, arithmetic and copies ran while one was open for 7% of the time, Pallas kernels for 2%

profile of v3, /device:TPU:2, one launch (start us, length us, event | category | flops | bytes accessed | tf_op | source)
XLA Modules:
  0.0 129.2 jit_solution(8967445162569244632)
XLA Ops:
  6.6 4.0 %collective-permute-done = bf16[48,768]{1,0:T(8,128)(2,1)S(1)} collective-permute-done((bf16[48,768]{1,0:T(8,128)(2,1)}, bf16[48,768]{1,0:T(8,128)(2,1)S(1)}, u32[]{:S(2)}, u32[]{:S(2)}) %collective-permute-start) | collective-permute-done | bytes 73760 | tf_op jit(solution)/shard_map/ppermute | solution.py:28
  10.5 13.6 %all_gather.12 = bf16[192,768]{1,0:T(8,128)(2,1)} all-gather(bf16[48,768]{1,0:T(8,128)(2,1)S(1)} %collective-permute-done), channel_id=1, replica_groups={{0,16,32,48},{1,17,33,49},{2,18,34,50},{3,19,35,51},{4,20,36,52},{5,21,..., dimensions={0}, use_global_device_ids=true | all-gather | bytes 368640 | tf_op jit(solution)/shard_map/all_gather | solution.py:123
  24.1 0.0 all-gather.3.cloned.1.call-update
  24.1 1.3 dynamic-slice
  26.1 0.7 fusion.4
  26.8 0.7 broadcast_in_dim.54
  27.5 15.2 %all-to-all-start = ((bf16[16,8,768]{2,1,0:T(8,128)(2,1)}), bf16[16,8,768]{2,1,0:T(8,128)(2,1)S(1)}, u32[]{:S(2)}, u32[]{:S(2)}) async-start(bf16[16,8,768]{2,1,0:T(8,128)(2,1)} %broadcast_in_dim.54), calls=%async_computation | async-start | bytes 393216 | tf_op jit(solution)/shard_map/all_to_all | solution.py:147
  42.7 0.8 select_reduce_fusion.1
  43.5 0.7 add_select_fusion
  44.2 0.8 select_reduce_fusion
  45.0 0.8 add_dynamic-update-slice_fusion
  45.8 8.3 %all-reduce = s32[144]{0:T(256)S(1)} all-reduce(s32[144]{0:T(256)S(1)} %add_dynamic-update-slice_fusion), channel_id=2, replica_groups=mesh['segment'=8,'frames'=64] {'segment'}, use_global_device_ids=true, to_apply=%add | all-reduce | flops 144 | bytes 1152
  54.1 0.1 slice_bitcast_fusion
  54.2 0.4 multiply_reduce_fusion
  54.6 0.1 reshape.121
  54.7 0.1 constant_dynamic-slice_fusion
  54.8 0.1 slice_bitcast_fusion.1
  54.9 0.6 reshape.110.spot
  55.5 1.1 collective-permute-start.1
  56.6 2.2 %collective-permute-done.2 = f32[12,1536]{1,0:T(8,128)S(1)} collective-permute-done((f32[12,1536]{1,0:T(8,128)S(1)}, f32[12,1536]{1,0:T(8,128)S(1)}, u32[]{:S(2)}, u32[]{:S(2)}) %collective-permute-start.2) | collective-permute-done | bytes 73760 | tf_op jit(solution)/shard_map/ppermute | solution.py:28
  58.8 0.8 all-to-all-done
  59.6 14.9 %all_gather.14 = bf16[512,768]{1,0:T(8,128)(2,1)} all-gather(bf16[128,768]{1,0:T(8,128)(2,1)S(1)} %bitcast.44), channel_id=1, replica_groups={{0,16,32,48},{1,17,33,49},{2,18,34,50},{3,19,35,51},{4,20,36,52},{5,21,..., dimensions={0}, use_global_device_ids=true | all-gather | bytes 983040 | tf_op jit(solution)/shard_map/all_gather | solution.py:148
  74.5 2.2 %shard_map.73 = bf16[80,8,768]{2,1,0:T(8,128)(2,1)} custom-call(s32[80]{0:T(128)} %reshape.110.spot, bf16[64,8,768]{2,1,0:T(8,128)(2,1)} %bitcast.43), custom_call_target="tpu_custom_call" | custom-call | tf_op jit(solution)/shard_map/pallas_call | solution.py:112
  76.7 5.6 %all-to-all-start.1 = ((bf16[8,80,768]{2,1,0:T(8,128)(2,1)}), bf16[8,80,768]{2,1,0:T(8,128)(2,1)S(1)}, u32[]{:S(2)}, u32[]{:S(2)}) async-start(bf16[8,80,768]{2,1,0:T(8,128)(2,1)} %bitcast.42), calls=%async_computation.1 | async-start | bytes 1966080 | tf_op jit(solution)/shard_map/all_to_all | solution.py:150
  82.3 0.1 fusion.5
  82.4 0.2 fusion
  82.7 0.3 fusion.3.q_ref
  83.0 13.2 %all-to-all-done.1 = bf16[8,80,768]{2,1,0:T(8,128)(2,1)S(1)} async-done(((bf16[8,80,768]{2,1,0:T(8,128)(2,1)}), bf16[8,80,768]{2,1,0:T(8,128)(2,1)S(1)}, u32[]{:S(2)}, u32[]{:S(2)}) %all-to-all-start.1) | async-done | bytes 983072 | tf_op jit(solution)/shard_map/all_to_all | solution.py:150
  96.2 1.0 copy-done.1
  97.1 1.3 copy.12
  98.4 13.8 %all-gather.3.cloned.1.call-done = bf16[3072,768]{1,0:T(8,128)(2,1)} async-done(((bf16[192,768]{1,0:T(8,128)(2,1)}), bf16[3072,768]{1,0:T(8,128)(2,1)}) %all-gather.3.cloned.1.call-update) | async-done | bytes 4718608 | tf_op jit(solution)/shard_map/all_gather | solution.py:125
  112.2 10.2 %shard_map.74 = bf16[256,1536]{1,0:T(8,128)(2,1)} custom-call(s32[4]{0:T(128)S(1)} %broadcast_minimum_fusion.first, s32[4]{0:T(128)S(1)} %get-tuple-element.19.start, s32[4]{0:T(128)S(1)} %get-tuple-element.18.count, bf16[640,768]{1,0:T(8,128)(2,1)S(1)} %bitcast.38, bf16[256,1536]{1,0:T(8,128)(2,1)S(1)} %fusion.3.q_ref, ...), custom_call_target="tpu_custom_call" | custom-call | tf_op jit(solution)/shard_map/pallas_call | solution.py:90
  (21 shorter events, 0.2 us)
Async XLA Ops:
  6.5 20.3 %copy-start = (bf16[64,768]{1,0:T(8,128)(2,1)S(1)}, bf16[64,768]{1,0:T(8,128)(2,1)}, u32[]{:S(2)}) copy-start(bf16[64,768]{1,0:T(8,128)(2,1)} %param.8) | copy-start | bytes 294916
  6.5 47.7 %copy-start.2 = (f32[1,32,3,1536]{3,1,2,0:T(8,128)S(1)}, f32[1,32,3,1536]{3,1,2,0:T(8,128)}, u32[]{:S(2)}) copy-start(f32[1,32,3,1536]{3,1,2,0:T(8,128)} %param.10) | copy-start | bytes 1769476
  6.5 48.9 %copy-start.3 = (bf16[1,256,1536]{2,1,0:T(8,128)(2,1)S(1)}, bf16[1,256,1536]{2,1,0:T(8,128)(2,1)}, u32[]{:S(2)}) copy-start(bf16[1,256,1536]{2,1,0:T(8,128)(2,1)} %param.7) | copy-start | bytes 2359300
  6.5 105.7 %all-gather.3.cloned.1.call-start = ((), (), s32[]{:S(2)}) async-start(), calls=%async_computation.2 | async-start | bytes 5013504 | tf_op jit(solution)/shard_map/all_gather | solution.py:125
  6.5 4.0 %collective-permute-start = (bf16[48,768]{1,0:T(8,128)(2,1)}, bf16[48,768]{1,0:T(8,128)(2,1)S(1)}, u32[]{:S(2)}, u32[]{:S(2)}) collective-permute-start(bf16[48,768]{1,0:T(8,128)(2,1)} %bitcast.53), channel_id=1, source_target_pairs={{448,0},{0,64},{64,128},{128,192},{192,256},{256,320},{320,384},{3... | collective-permute-start | bytes 221192 | tf_op jit(solution)/shard_map/ppermute | solution.py:28
  27.5 32.1 %all-to-all-start = ((bf16[16,8,768]{2,1,0:T(8,128)(2,1)}), bf16[16,8,768]{2,1,0:T(8,128)(2,1)S(1)}, u32[]{:S(2)}, u32[]{:S(2)}) async-start(bf16[16,8,768]{2,1,0:T(8,128)(2,1)} %broadcast_in_dim.54), calls=%async_computation | async-start | bytes 393216 | tf_op jit(solution)/shard_map/all_to_all | solution.py:147
  54.7 4.1 %collective-permute-start.2 = (f32[12,1536]{1,0:T(8,128)S(1)}, f32[12,1536]{1,0:T(8,128)S(1)}, u32[]{:S(2)}, u32[]{:S(2)}) collective-permute-start(f32[12,1536]{1,0:T(8,128)S(1)} %reshape.116), channel_id=1, source_target_pairs={{448,0},{0,64},{64,128},{128,192},{192,256},{256,320},{320,384},{3... | collective-permute-start | bytes 221192 | tf_op jit(solution)/shard_map/ppermute | solution.py:28
  55.5 26.9 %collective-permute-start.1 = (bf16[256,1536]{1,0:T(8,128)(2,1)S(1)}, bf16[256,1536]{1,0:T(8,128)(2,1)S(1)}, u32[]{:S(2)}, u32[]{:S(2)}) collective-permute-start(bf16[256,1536]{1,0:T(8,128)(2,1)S(1)} %bitcast.52), channel_id=1, source_target_pairs={{448,0},{0,64},{64,128},{128,192},{192,256},{256,320},{320,384},{3... | collective-permute-start | bytes 2359304 | tf_op jit(solution)/shard_map/ppermute | solution.py:28
  76.7 19.5 %all-to-all-start.1 = ((bf16[8,80,768]{2,1,0:T(8,128)(2,1)}), bf16[8,80,768]{2,1,0:T(8,128)(2,1)S(1)}, u32[]{:S(2)}, u32[]{:S(2)}) async-start(bf16[8,80,768]{2,1,0:T(8,128)(2,1)} %bitcast.42), calls=%async_computation.1 | async-start | bytes 1966080 | tf_op jit(solution)/shard_map/all_to_all | solution.py:150
  96.2 1.0 copy-start.1
Sparse Core Ops, SparseCore 0:
  24.3 87.8 all-gather.2

commit v4 on v3

--- a/solution.py
+++ b/solution.py
@@ -31,7 +31,7 @@
 def attend(first, start, count, x_ref, q_ref, hid_ref, gate_ref, w_ref, out_ref, wv, kv, sem):
     copies = []
     for i, part in enumerate((0, 2, 1, 3)):
-        copy = pltpu.make_async_copy(w_ref.at[:, part], wv.at[part], sem.at[i])
+        copy = pltpu.make_async_copy(w_ref.at[:, part], wv.at[i], sem.at[i])
         copy.start()
         copies.append(copy)
     inv_root = 1.0 / HD**0.5
@@ -41,29 +41,30 @@
     def heads_of(half, b):
         rows = slice(b * BLK, (b + 1) * BLK)
         for h in range(HEADS // 2):
+            keys = 2 * half * HALF + h * HD
             cols = slice(half * HALF + h * HD, half * HALF + (h + 1) * HD)
-            yield rows, cols, slice(h * HD, (h + 1) * HD)
+            yield rows, cols, slice(keys, keys + HD), slice(keys + HALF, keys + HALF + HD)
 
     def scores_of(half, b):
         return [
             lax.dot_general(
                 q_ref[rows, cols],
-                kv[half, windows[b], inner],
+                kv[windows[b], keys],
                 (((1,), (1,)), ((), ())),
                 preferred_element_type=jnp.float32,
             )
-            for rows, cols, inner in heads_of(half, b)
+            for rows, cols, keys, _ in heads_of(half, b)
         ]
 
     for half in range(2):
-        for i, part in ((2 * half, half), (2 * half + 1, half + 2)):
-            copies[i].wait()
-            kv[part] = lax.dot_general(
-                x_ref[...],
-                wv[part].reshape(Z * COLS, FW),
-                (((1,), (1,)), ((), ())),
-                preferred_element_type=jnp.float32,
-            ).astype(jnp.bfloat16)
+        for copy in copies[2 * half : 2 * half + 2]:
+            copy.wait()
+        kv[:, half * DW : (half + 1) * DW] = lax.dot_general(
+            x_ref[...],
+            wv[2 * half : 2 * half + 2].reshape(DW, FW),
+            (((1,), (1,)), ((), ())),
+            preferred_element_type=jnp.float32,
+        ).astype(jnp.bfloat16)
         ahead = scores_of(half, 0)
         for b in range(4):
             scores = ahead
@@ -76,10 +77,8 @@
                 score = jnp.where(mask, score * inv_root, jnp.float32(-1e30))
                 expo = jnp.exp(score - jnp.max(score, axis=-1, keepdims=True))
                 weights.append((expo / jnp.sum(expo, axis=-1, keepdims=True)).astype(jnp.bfloat16))
-            for weight, (rows, cols, inner) in zip(weights, heads_of(half, b)):
-                mixed = jnp.dot(
-                    weight, kv[half + 2, windows[b], inner], preferred_element_type=jnp.float32
-                )
+            for weight, (rows, cols, _, vals) in zip(weights, heads_of(half, b)):
+                mixed = jnp.dot(weight, kv[windows[b], vals], preferred_element_type=jnp.float32)
                 out_ref[rows, cols] = (
                     hid_ref[rows, cols].astype(jnp.float32) + gate_ref[b : b + 1, cols] * mixed
                 ).astype(jnp.bfloat16)
@@ -95,7 +94,7 @@
         out_specs=whole(),
         scratch_shapes=[
             pltpu.VMEM((Y, Z, COLS, FW), jnp.bfloat16),
-            pltpu.VMEM((Y, LIVE * BLK, HALF), jnp.bfloat16),
+            pltpu.VMEM((LIVE * BLK, 2 * DW), jnp.bfloat16),
             pltpu.SemaphoreType.DMA((4,)),
         ],
         compiler_params=pltpu.CompilerParams(vmem_limit_bytes=40 * 1024 * 1024),
@@ -120,8 +119,10 @@
 def local(hidden, features, kv_weight, mod_table, timestep, block_list, block_count):
     me = lax.axis_index("segment")
     slab = from_behind(kv_weight[0].T, "segment", 1)
-    slab = lax.all_gather(slab, "frames", axis=0, tiled=True, axis_index_groups=Y_GROUPS)
-    features, slab, block_count, mod_table, hidden = lax.optimization_barrier((features, slab, block_count, mod_table, hidden))
+    slab = lax.all_to_all(
+        jnp.broadcast_to(slab[None], (Y, COLS, FW)), "frames", 0, 0, axis_index_groups=Y_GROUPS
+    ).reshape(Y * COLS, FW)
+    slab, block_count, mod_table, hidden = lax.optimization_barrier((slab, block_count, mod_table, hidden))
     weight = lax.all_gather(slab, "frames", axis=0, tiled=True, axis_index_groups=Z_GROUPS)
     stream_in = from_behind(hidden[0], "segment", 1)
     levels = mod_table.shape[1]

time: 130 us -> 124 us (0.954)
  the two profiles are of different devices: /device:TPU:2 before, /device:TPU:4 now
where the time goes in v4:
time: 124 us; the launch traced here: 123 us
  waiting for transfers between devices  34.6 us (28%)
  blocking collectives  33.7 us (27%)
  starting transfers between devices  22.5 us (18%)
  between operations  14.2 us (11%)
  Pallas kernels  11.5 us (9%)
  local copies, waits for them, and re-layouts  5.3 us (4%)
  other arithmetic  1.51 us (1%)
    all_gather x1, waiting for transfers between devices, local(): lax.all_gather(slab, 'frames', axis=0, tiled=True, axis_index_groups=Z_GR...  17.2 us
    all_to_all x1, starting transfers between devices, local(): lax.all_to_all(jnp.broadcast_to(part[None], (Z, PART, FW)), 'frames', 0,...  15.2 us
    all_gather x1, blocking collectives, local(): lax.all_gather(table.reshape(Z * PART, FW), 'frames', axis=0, tiled=True,...  14.9 us
    all_to_all x1, waiting for transfers between devices, local(): lax.all_to_all(picked.reshape(SEG, LIVE * PART, FW), 'segment', 0, 0)  11.4 us
    all_to_all x1, blocking collectives, local(): lax.all_to_all(jnp.broadcast_to(slab[None], (Y, COLS, FW)), 'frames', 0,...  11.2 us
    pallas_call x1, Pallas kernels, attention(): pl.pallas_call(attend, out_shape=jax.ShapeDtypeStruct((4 * BLK, DW), jnp....  9.26 us
    unnamed x1, blocking collectives  7.57 us
    all_to_all x1, starting transfers between devices, local(): lax.all_to_all(picked.reshape(SEG, LIVE * PART, FW), 'segment', 0, 0)  5.37 us
  transfers between devices with their start and end apart: 6, of which 5 were waited for; matrix products, arithmetic and copies ran while one was open for 5% of the time, Pallas kernels for 2%

profile of v4, /device:TPU:4, one launch (start us, length us, event | category | flops | bytes accessed | tf_op | source)
XLA Modules:
  0.0 123.3 jit_solution(13751267744739484993)
XLA Ops:
  6.6 0.0 all-gather.3.cloned.1.call-start
  6.6 4.0 %collective-permute-done = bf16[48,768]{1,0:T(8,128)(2,1)S(1)} collective-permute-done((bf16[48,768]{1,0:T(8,128)(2,1)}, bf16[48,768]{1,0:T(8,128)(2,1)S(1)}, u32[]{:S(2)}, u32[]{:S(2)}) %collective-permute-start) | collective-permute-done | bytes 73760 | tf_op jit(solution)/shard_map/ppermute | solution.py:28
  10.6 11.2 %all_to_all.15 = bf16[4,48,768]{2,1,0:T(8,128)(2,1)} all-to-all(bf16[4,48,768]{2,1,0:T(8,128)(2,1)S(1)} %broadcast_in_dim.54), channel_id=1, replica_groups={{0,16,32,48},{1,17,33,49},{2,18,34,50},{3,19,35,51},{4,20,36,52},{5,21,..., dimensions={0} | all-to-all | bytes 589824 | tf_op jit(solution)/shard_map/all_to_all | solution.py:122
  21.9 0.7 broadcast_in_dim.61
  22.6 15.2 %all-to-all-start.1 = ((bf16[16,8,768]{2,1,0:T(8,128)(2,1)}), bf16[16,8,768]{2,1,0:T(8,128)(2,1)S(1)}, u32[]{:S(2)}, u32[]{:S(2)}) async-start(bf16[16,8,768]{2,1,0:T(8,128)(2,1)} %broadcast_in_dim.61), calls=%async_computation.1 | async-start | bytes 393216 | tf_op jit(solution)/shard_map/all_to_all | solution.py:148
  37.8 1.3 %dynamic-slice = u32[1]{0:T(128)} dynamic-slice(u32[512]{0:T(512)} %constant.35, u32[]{:T(128)S(6)} %add.63), dynamic_slice_sizes={1} | dynamic-slice | bytes 12
  39.8 0.1 fusion.4
  39.8 0.1 select_reduce_fusion.1
  39.9 0.1 add_select_fusion
  40.0 0.1 select_reduce_fusion
  40.1 0.2 add_dynamic-update-slice_fusion
  40.3 7.6 %all-reduce = s32[144]{0:T(256)S(1)} all-reduce(s32[144]{0:T(256)S(1)} %add_dynamic-update-slice_fusion), channel_id=2, replica_groups=mesh['segment'=8,'frames'=64] {'segment'}, use_global_device_ids=true, to_apply=%add | all-reduce | flops 144 | bytes 1152
  47.9 0.1 slice_bitcast_fusion
  48.0 0.4 multiply_reduce_fusion
  48.3 0.1 reshape.126
  48.5 0.1 constant_dynamic-slice_fusion
  48.6 0.1 slice_bitcast_fusion.1
  48.6 0.6 reshape.115.spot
  49.2 1.9 %collective-permute-start.1 = (bf16[256,1536]{1,0:T(8,128)(2,1)S(1)}, bf16[256,1536]{1,0:T(8,128)(2,1)S(1)}, u32[]{:S(2)}, u32[]{:S(2)}) collective-permute-start(bf16[256,1536]{1,0:T(8,128)(2,1)S(1)} %bitcast.54), channel_id=1, source_target_pairs={{448,0},{0,64},{64,128},{128,192},{192,256},{256,320},{320,384},{3... | collective-permute-start | bytes 2359304 | tf_op jit(solution)/shard_map/ppermute | solution.py:28
  51.1 1.4 %collective-permute-done.2 = f32[12,1536]{1,0:T(8,128)S(1)} collective-permute-done((f32[12,1536]{1,0:T(8,128)S(1)}, f32[12,1536]{1,0:T(8,128)S(1)}, u32[]{:S(2)}, u32[]{:S(2)}) %collective-permute-start.2) | collective-permute-done | bytes 73760 | tf_op jit(solution)/shard_map/ppermute | solution.py:28
  52.5 0.6 all-to-all-done.1
  53.1 14.9 %all_gather.10 = bf16[512,768]{1,0:T(8,128)(2,1)} all-gather(bf16[128,768]{1,0:T(8,128)(2,1)S(1)} %bitcast.46), channel_id=1, replica_groups={{0,16,32,48},{1,17,33,49},{2,18,34,50},{3,19,35,51},{4,20,36,52},{5,21,..., dimensions={0}, use_global_device_ids=true | all-gather | bytes 983040 | tf_op jit(solution)/shard_map/all_gather | solution.py:149
  68.1 2.2 %shard_map.73 = bf16[80,8,768]{2,1,0:T(8,128)(2,1)} custom-call(s32[80]{0:T(128)} %reshape.115.spot, bf16[64,8,768]{2,1,0:T(8,128)(2,1)} %bitcast.44), custom_call_target="tpu_custom_call" | custom-call | tf_op jit(solution)/shard_map/pallas_call | solution.py:111
  70.3 5.4 %all-to-all-start.2 = ((bf16[8,80,768]{2,1,0:T(8,128)(2,1)}), bf16[8,80,768]{2,1,0:T(8,128)(2,1)S(1)}, u32[]{:S(2)}, u32[]{:S(2)}) async-start(bf16[8,80,768]{2,1,0:T(8,128)(2,1)} %bitcast.43), calls=%async_computation.2 | async-start | bytes 1966080 | tf_op jit(solution)/shard_map/all_to_all | solution.py:151
  75.7 0.1 fusion.5
  75.8 0.2 fusion
  76.0 0.3 fusion.3.q_ref
  76.3 11.4 %all-to-all-done.2 = bf16[8,80,768]{2,1,0:T(8,128)(2,1)S(1)} async-done(((bf16[8,80,768]{2,1,0:T(8,128)(2,1)}), bf16[8,80,768]{2,1,0:T(8,128)(2,1)S(1)}, u32[]{:S(2)}, u32[]{:S(2)}) %all-to-all-start.2) | async-done | bytes 983072 | tf_op jit(solution)/shard_map/all_to_all | solution.py:151
  87.8 1.0 copy-done.1
  88.8 1.3 %copy.12 = bf16[10,8,8,768]{3,2,1,0:T(8,128)(2,1)S(1)} copy(bf16[10,8,8,768]{3,2,0,1:T(8,128)(2,1)} %bitcast.42) | data formatting | bytes 1966080 | tf_op jit(solution)/shard_map/transpose | solution.py:152
  90.0 17.2 %all-gather.3.cloned.1.call-done = bf16[3072,768]{1,0:T(8,128)(2,1)} async-done(((bf16[192,768]{1,0:T(8,128)(2,1)}), bf16[3072,768]{1,0:T(8,128)(2,1)}) %all-gather.3.cloned.1.call-update) | async-done | bytes 4718608 | tf_op jit(solution)/shard_map/all_gather | solution.py:126
  107.2 9.3 %shard_map.74 = bf16[256,1536]{1,0:T(8,128)(2,1)} custom-call(s32[4]{0:T(128)S(1)} %broadcast_minimum_fusion.first, s32[4]{0:T(128)S(1)} %get-tuple-element.17.start, s32[4]{0:T(128)S(1)} %get-tuple-element.16.count, bf16[640,768]{1,0:T(8,128)(2,1)S(1)} %bitcast.39, bf16[256,1536]{1,0:T(8,128)(2,1)S(1)} %fusion.3.q_ref, ...), custom_call_target="tpu_custom_call" | custom-call | tf_op jit(solution)/shard_map/pallas_call | solution.py:89
  (28 shorter events, 0.2 us)
Async XLA Ops:
  6.5 15.4 %copy-start = (bf16[64,768]{1,0:T(8,128)(2,1)S(1)}, bf16[64,768]{1,0:T(8,128)(2,1)}, u32[]{:S(2)}) copy-start(bf16[64,768]{1,0:T(8,128)(2,1)} %param.8) | copy-start | bytes 294916
  6.5 33.3 %copy-start.4 = (s32[1,4]{1,0:T(1,128)S(1)}, s32[1,4]{1,0:T(1,128)}, u32[]{:S(2)}) copy-start(s32[1,4]{1,0:T(1,128)} %param.13) | copy-start | bytes 52
  6.5 41.4 %copy-start.2 = (f32[1,32,3,1536]{3,1,2,0:T(8,128)S(1)}, f32[1,32,3,1536]{3,1,2,0:T(8,128)}, u32[]{:S(2)}) copy-start(f32[1,32,3,1536]{3,1,2,0:T(8,128)} %param.10) | copy-start | bytes 1769476
  6.5 42.7 %copy-start.6 = (bf16[1,256,1536]{2,1,0:T(8,128)(2,1)S(1)}, bf16[1,256,1536]{2,1,0:T(8,128)(2,1)}, u32[]{:S(2)}) copy-start(bf16[1,256,1536]{2,1,0:T(8,128)(2,1)} %param.7) | copy-start | bytes 2359300
  6.5 33.2 %copy-start.5 = (s32[1,4]{1,0:T(1,128)S(1)}, s32[1,4]{1,0:T(1,128)}, u32[]{:S(2)}) copy-start(s32[1,4]{1,0:T(1,128)} %param.11) | copy-start | bytes 52
  6.5 33.5 %copy-start.3 = (s32[1,4,4]{2,1,0:T(4,128)S(1)}, s32[1,4,4]{2,1,0:T(4,128)}, u32[]{:S(2)}) copy-start(s32[1,4,4]{2,1,0:T(4,128)} %param.12) | copy-start | bytes 196
  6.6 100.7 %all-gather.3.cloned.1.call-start = ((), (), s32[]{:S(2)}) async-start(), calls=%async_computation.3 | async-start | bytes 5013504 | tf_op jit(solution)/shard_map/all_gather | solution.py:126
  6.6 4.0 %collective-permute-start = (bf16[48,768]{1,0:T(8,128)(2,1)}, bf16[48,768]{1,0:T(8,128)(2,1)S(1)}, u32[]{:S(2)}, u32[]{:S(2)}) collective-permute-start(bf16[48,768]{1,0:T(8,128)(2,1)} %bitcast.55), channel_id=1, source_target_pairs={{448,0},{0,64},{64,128},{128,192},{192,256},{256,320},{320,384},{3... | collective-permute-start | bytes 221192 | tf_op jit(solution)/shard_map/ppermute | solution.py:28
  22.6 30.5 %all-to-all-start.1 = ((bf16[16,8,768]{2,1,0:T(8,128)(2,1)}), bf16[16,8,768]{2,1,0:T(8,128)(2,1)S(1)}, u32[]{:S(2)}, u32[]{:S(2)}) async-start(bf16[16,8,768]{2,1,0:T(8,128)(2,1)} %broadcast_in_dim.61), calls=%async_computation.1 | async-start | bytes 393216 | tf_op jit(solution)/shard_map/all_to_all | solution.py:148
  48.4 4.1 %collective-permute-start.2 = (f32[12,1536]{1,0:T(8,128)S(1)}, f32[12,1536]{1,0:T(8,128)S(1)}, u32[]{:S(2)}, u32[]{:S(2)}) collective-permute-start(f32[12,1536]{1,0:T(8,128)S(1)} %reshape.121), channel_id=1, source_target_pairs={{448,0},{0,64},{64,128},{128,192},{192,256},{256,320},{320,384},{3... | collective-permute-start | bytes 221192 | tf_op jit(solution)/shard_map/ppermute | solution.py:28
  49.2 26.5 %collective-permute-start.1 = (bf16[256,1536]{1,0:T(8,128)(2,1)S(1)}, bf16[256,1536]{1,0:T(8,128)(2,1)S(1)}, u32[]{:S(2)}, u32[]{:S(2)}) collective-permute-start(bf16[256,1536]{1,0:T(8,128)(2,1)S(1)} %bitcast.54), channel_id=1, source_target_pairs={{448,0},{0,64},{64,128},{128,192},{192,256},{256,320},{320,384},{3... | collective-permute-start | bytes 2359304 | tf_op jit(solution)/shard_map/ppermute | solution.py:28
  70.3 17.5 %all-to-all-start.2 = ((bf16[8,80,768]{2,1,0:T(8,128)(2,1)}), bf16[8,80,768]{2,1,0:T(8,128)(2,1)S(1)}, u32[]{:S(2)}, u32[]{:S(2)}) async-start(bf16[8,80,768]{2,1,0:T(8,128)(2,1)} %bitcast.43), calls=%async_computation.2 | async-start | bytes 1966080 | tf_op jit(solution)/shard_map/all_to_all | solution.py:151
  87.8 1.0 copy-start.1
Sparse Core Ops, SparseCore 0:
  22.0 85.1 all-gather.2

commit v5 on v4

--- a/solution.py
+++ b/solution.py
@@ -28,7 +28,7 @@
     return lax.ppermute(block, axis, route)
 
 
-def attend(first, start, count, x_ref, q_ref, hid_ref, gate_ref, w_ref, out_ref, wv, kv, sem):
+def attend(first, start, count, x_ref, q_ref, hid_ref, gate_ref, w_ref, out_ref, wv, kv, held, sem, out_sem):
     copies = []
     for i, part in enumerate((0, 2, 1, 3)):
         copy = pltpu.make_async_copy(w_ref.at[:, part], wv.at[i], sem.at[i])
@@ -56,6 +56,7 @@
             for rows, cols, keys, _ in heads_of(half, b)
         ]
 
+    sent = []
     for half in range(2):
         for copy in copies[2 * half : 2 * half + 2]:
             copy.wait()
@@ -79,9 +80,16 @@
                 weights.append((expo / jnp.sum(expo, axis=-1, keepdims=True)).astype(jnp.bfloat16))
             for weight, (rows, cols, _, vals) in zip(weights, heads_of(half, b)):
                 mixed = jnp.dot(weight, kv[windows[b], vals], preferred_element_type=jnp.float32)
-                out_ref[rows, cols] = (
+                held[rows, cols] = (
                     hid_ref[rows, cols].astype(jnp.float32) + gate_ref[b : b + 1, cols] * mixed
                 ).astype(jnp.bfloat16)
+            if half == 1:
+                done = slice(b * BLK, (b + 1) * BLK)
+                copy = pltpu.make_async_copy(held.at[done], out_ref.at[done], out_sem.at[b])
+                copy.start()
+                sent.append(copy)
+    for copy in sent:
+        copy.wait()
 
 
 def attention(first, start, count, x, q, hidden, gate, w):
@@ -91,10 +99,12 @@
         out_shape=jax.ShapeDtypeStruct((4 * BLK, DW), jnp.bfloat16),
         in_specs=[pl.BlockSpec(memory_space=pltpu.SMEM)] * 3
         + [whole(), whole(), whole(), whole(), pl.BlockSpec(memory_space=pltpu.HBM)],
-        out_specs=whole(),
+        out_specs=pl.BlockSpec(memory_space=pltpu.HBM),
         scratch_shapes=[
             pltpu.VMEM((Y, Z, COLS, FW), jnp.bfloat16),
             pltpu.VMEM((LIVE * BLK, 2 * DW), jnp.bfloat16),
+            pltpu.VMEM((4 * BLK, DW), jnp.bfloat16),
+            pltpu.SemaphoreType.DMA((4,)),
             pltpu.SemaphoreType.DMA((4,)),
         ],
         compiler_params=pltpu.CompilerParams(vmem_limit_bytes=40 * 1024 * 1024),

time: 124 us -> 124 us (level)
  no operation moved by 1% of the time
where the time goes in v5:
time: 124 us; the launch traced here: 123 us
  waiting for transfers between devices  34.6 us (28%)
  blocking collectives  33.7 us (27%)
  starting transfers between devices  22.5 us (18%)
  between operations  14.2 us (11%)
  Pallas kernels  11.3 us (9%)
  local copies, waits for them, and re-layouts  5.3 us (4%)
  other arithmetic  1.51 us (1%)
    all_gather x1, waiting for transfers between devices, local(): lax.all_gather(slab, 'frames', axis=0, tiled=True, axis_index_groups=Z_GR...  17.2 us
    all_to_all x1, starting transfers between devices, local(): lax.all_to_all(jnp.broadcast_to(part[None], (Z, PART, FW)), 'frames', 0,...  15.2 us
    all_gather x1, blocking collectives, local(): lax.all_gather(table.reshape(Z * PART, FW), 'frames', axis=0, tiled=True,...  14.9 us
    all_to_all x1, waiting for transfers between devices, local(): lax.all_to_all(picked.reshape(SEG, LIVE * PART, FW), 'segment', 0, 0)  11.4 us
    all_to_all x1, blocking collectives, local(): lax.all_to_all(jnp.broadcast_to(slab[None], (Y, COLS, FW)), 'frames', 0,...  11.2 us
    pallas_call x1, Pallas kernels, attention(): pl.pallas_call(attend, out_shape=jax.ShapeDtypeStruct((4 * BLK, DW), jnp....  9.1 us
    unnamed x1, blocking collectives  7.57 us
    all_to_all x1, starting transfers between devices, local(): lax.all_to_all(picked.reshape(SEG, LIVE * PART, FW), 'segment', 0, 0)  5.37 us
  transfers between devices with their start and end apart: 6, of which 5 were waited for; matrix products, arithmetic and copies ran while one was open for 5% of the time, Pallas kernels for 2%

profile of v5, /device:TPU:4, one launch (start us, length us, event | category | flops | bytes accessed | tf_op | source)
XLA Modules:
  0.0 123.2 jit_solution(7207500654128174176)
XLA Ops:
  6.6 0.0 all-gather.3.cloned.1.call-start
  6.6 4.0 %collective-permute-done = bf16[48,768]{1,0:T(8,128)(2,1)S(1)} collective-permute-done((bf16[48,768]{1,0:T(8,128)(2,1)}, bf16[48,768]{1,0:T(8,128)(2,1)S(1)}, u32[]{:S(2)}, u32[]{:S(2)}) %collective-permute-start) | collective-permute-done | bytes 73760 | tf_op jit(solution)/shard_map/ppermute | solution.py:28
  10.6 11.2 %all_to_all.15 = bf16[4,48,768]{2,1,0:T(8,128)(2,1)} all-to-all(bf16[4,48,768]{2,1,0:T(8,128)(2,1)S(1)} %broadcast_in_dim.54), channel_id=1, replica_groups={{0,16,32,48},{1,17,33,49},{2,18,34,50},{3,19,35,51},{4,20,36,52},{5,21,..., dimensions={0} | all-to-all | bytes 589824 | tf_op jit(solution)/shard_map/all_to_all | solution.py:132
  21.9 0.7 broadcast_in_dim.61
  22.6 15.2 %all-to-all-start.1 = ((bf16[16,8,768]{2,1,0:T(8,128)(2,1)}), bf16[16,8,768]{2,1,0:T(8,128)(2,1)S(1)}, u32[]{:S(2)}, u32[]{:S(2)}) async-start(bf16[16,8,768]{2,1,0:T(8,128)(2,1)} %broadcast_in_dim.61), calls=%async_computation.1 | async-start | bytes 393216 | tf_op jit(solution)/shard_map/all_to_all | solution.py:158
  37.8 1.3 %dynamic-slice = u32[1]{0:T(128)} dynamic-slice(u32[512]{0:T(512)} %constant.35, u32[]{:T(128)S(6)} %add.63), dynamic_slice_sizes={1} | dynamic-slice | bytes 12
  39.8 0.1 fusion.4
  39.8 0.1 select_reduce_fusion.1
  39.9 0.1 add_select_fusion
  40.0 0.1 select_reduce_fusion
  40.1 0.2 add_dynamic-update-slice_fusion
  40.3 7.6 %all-reduce = s32[144]{0:T(256)S(1)} all-reduce(s32[144]{0:T(256)S(1)} %add_dynamic-update-slice_fusion), channel_id=2, replica_groups=mesh['segment'=8,'frames'=64] {'segment'}, use_global_device_ids=true, to_apply=%add | all-reduce | flops 144 | bytes 1152
  47.9 0.1 slice_bitcast_fusion
  48.0 0.4 multiply_reduce_fusion
  48.3 0.1 reshape.126
  48.5 0.1 constant_dynamic-slice_fusion
  48.6 0.1 slice_bitcast_fusion.1
  48.6 0.6 reshape.115.spot
  49.2 1.9 %collective-permute-start.1 = (bf16[256,1536]{1,0:T(8,128)(2,1)S(1)}, bf16[256,1536]{1,0:T(8,128)(2,1)S(1)}, u32[]{:S(2)}, u32[]{:S(2)}) collective-permute-start(bf16[256,1536]{1,0:T(8,128)(2,1)S(1)} %bitcast.54), channel_id=1, source_target_pairs={{448,0},{0,64},{64,128},{128,192},{192,256},{256,320},{320,384},{3... | collective-permute-start | bytes 2359304 | tf_op jit(solution)/shard_map/ppermute | solution.py:28
  51.1 1.4 %collective-permute-done.2 = f32[12,1536]{1,0:T(8,128)S(1)} collective-permute-done((f32[12,1536]{1,0:T(8,128)S(1)}, f32[12,1536]{1,0:T(8,128)S(1)}, u32[]{:S(2)}, u32[]{:S(2)}) %collective-permute-start.2) | collective-permute-done | bytes 73760 | tf_op jit(solution)/shard_map/ppermute | solution.py:28
  52.5 0.6 all-to-all-done.1
  53.1 14.9 %all_gather.10 = bf16[512,768]{1,0:T(8,128)(2,1)} all-gather(bf16[128,768]{1,0:T(8,128)(2,1)S(1)} %bitcast.46), channel_id=1, replica_groups={{0,16,32,48},{1,17,33,49},{2,18,34,50},{3,19,35,51},{4,20,36,52},{5,21,..., dimensions={0}, use_global_device_ids=true | all-gather | bytes 983040 | tf_op jit(solution)/shard_map/all_gather | solution.py:159
  68.1 2.2 %shard_map.73 = bf16[80,8,768]{2,1,0:T(8,128)(2,1)} custom-call(s32[80]{0:T(128)} %reshape.115.spot, bf16[64,8,768]{2,1,0:T(8,128)(2,1)} %bitcast.44), custom_call_target="tpu_custom_call" | custom-call | tf_op jit(solution)/shard_map/pallas_call | solution.py:121
  70.3 5.4 %all-to-all-start.2 = ((bf16[8,80,768]{2,1,0:T(8,128)(2,1)}), bf16[8,80,768]{2,1,0:T(8,128)(2,1)S(1)}, u32[]{:S(2)}, u32[]{:S(2)}) async-start(bf16[8,80,768]{2,1,0:T(8,128)(2,1)} %bitcast.43), calls=%async_computation.2 | async-start | bytes 1966080 | tf_op jit(solution)/shard_map/all_to_all | solution.py:161
  75.7 0.1 fusion.5
  75.8 0.2 fusion
  76.0 0.3 fusion.3.q_ref
  76.3 11.4 %all-to-all-done.2 = bf16[8,80,768]{2,1,0:T(8,128)(2,1)S(1)} async-done(((bf16[8,80,768]{2,1,0:T(8,128)(2,1)}), bf16[8,80,768]{2,1,0:T(8,128)(2,1)S(1)}, u32[]{:S(2)}, u32[]{:S(2)}) %all-to-all-start.2) | async-done | bytes 983072 | tf_op jit(solution)/shard_map/all_to_all | solution.py:161
  87.8 1.0 copy-done.1
  88.8 1.3 %copy.12 = bf16[10,8,8,768]{3,2,1,0:T(8,128)(2,1)S(1)} copy(bf16[10,8,8,768]{3,2,0,1:T(8,128)(2,1)} %bitcast.42) | data formatting | bytes 1966080 | tf_op jit(solution)/shard_map/transpose | solution.py:162
  90.0 17.2 %all-gather.3.cloned.1.call-done = bf16[3072,768]{1,0:T(8,128)(2,1)} async-done(((bf16[192,768]{1,0:T(8,128)(2,1)}), bf16[3072,768]{1,0:T(8,128)(2,1)}) %all-gather.3.cloned.1.call-update) | async-done | bytes 4718608 | tf_op jit(solution)/shard_map/all_gather | solution.py:136
  107.2 9.1 %shard_map.74 = bf16[256,1536]{1,0:T(8,128)(2,1)} custom-call(s32[4]{0:T(128)S(1)} %broadcast_minimum_fusion.first, s32[4]{0:T(128)S(1)} %get-tuple-element.17.start, s32[4]{0:T(128)S(1)} %get-tuple-element.16.count, bf16[640,768]{1,0:T(8,128)(2,1)S(1)} %bitcast.39, bf16[256,1536]{1,0:T(8,128)(2,1)S(1)} %fusion.3.q_ref, ...), custom_call_target="tpu_custom_call" | custom-call | tf_op jit(solution)/shard_map/pallas_call | solution.py:97
  (28 shorter events, 0.2 us)
Async XLA Ops:
  6.5 15.4 %copy-start = (bf16[64,768]{1,0:T(8,128)(2,1)S(1)}, bf16[64,768]{1,0:T(8,128)(2,1)}, u32[]{:S(2)}) copy-start(bf16[64,768]{1,0:T(8,128)(2,1)} %param.8) | copy-start | bytes 294916
  6.5 33.3 %copy-start.4 = (s32[1,4]{1,0:T(1,128)S(1)}, s32[1,4]{1,0:T(1,128)}, u32[]{:S(2)}) copy-start(s32[1,4]{1,0:T(1,128)} %param.13) | copy-start | bytes 52
  6.5 41.4 %copy-start.2 = (f32[1,32,3,1536]{3,1,2,0:T(8,128)S(1)}, f32[1,32,3,1536]{3,1,2,0:T(8,128)}, u32[]{:S(2)}) copy-start(f32[1,32,3,1536]{3,1,2,0:T(8,128)} %param.10) | copy-start | bytes 1769476
  6.5 42.7 %copy-start.6 = (bf16[1,256,1536]{2,1,0:T(8,128)(2,1)S(1)}, bf16[1,256,1536]{2,1,0:T(8,128)(2,1)}, u32[]{:S(2)}) copy-start(bf16[1,256,1536]{2,1,0:T(8,128)(2,1)} %param.7) | copy-start | bytes 2359300
  6.5 33.2 %copy-start.5 = (s32[1,4]{1,0:T(1,128)S(1)}, s32[1,4]{1,0:T(1,128)}, u32[]{:S(2)}) copy-start(s32[1,4]{1,0:T(1,128)} %param.11) | copy-start | bytes 52
  6.5 33.5 %copy-start.3 = (s32[1,4,4]{2,1,0:T(4,128)S(1)}, s32[1,4,4]{2,1,0:T(4,128)}, u32[]{:S(2)}) copy-start(s32[1,4,4]{2,1,0:T(4,128)} %param.12) | copy-start | bytes 196
  6.6 100.7 %all-gather.3.cloned.1.call-start = ((), (), s32[]{:S(2)}) async-start(), calls=%async_computation.3 | async-start | bytes 5013504 | tf_op jit(solution)/shard_map/all_gather | solution.py:136
  6.6 4.0 %collective-permute-start = (bf16[48,768]{1,0:T(8,128)(2,1)}, bf16[48,768]{1,0:T(8,128)(2,1)S(1)}, u32[]{:S(2)}, u32[]{:S(2)}) collective-permute-start(bf16[48,768]{1,0:T(8,128)(2,1)} %bitcast.55), channel_id=1, source_target_pairs={{448,0},{0,64},{64,128},{128,192},{192,256},{256,320},{320,384},{3... | collective-permute-start | bytes 221192 | tf_op jit(solution)/shard_map/ppermute | solution.py:28
  22.6 30.5 %all-to-all-start.1 = ((bf16[16,8,768]{2,1,0:T(8,128)(2,1)}), bf16[16,8,768]{2,1,0:T(8,128)(2,1)S(1)}, u32[]{:S(2)}, u32[]{:S(2)}) async-start(bf16[16,8,768]{2,1,0:T(8,128)(2,1)} %broadcast_in_dim.61), calls=%async_computation.1 | async-start | bytes 393216 | tf_op jit(solution)/shard_map/all_to_all | solution.py:158
  48.4 4.1 %collective-permute-start.2 = (f32[12,1536]{1,0:T(8,128)S(1)}, f32[12,1536]{1,0:T(8,128)S(1)}, u32[]{:S(2)}, u32[]{:S(2)}) collective-permute-start(f32[12,1536]{1,0:T(8,128)S(1)} %reshape.121), channel_id=1, source_target_pairs={{448,0},{0,64},{64,128},{128,192},{192,256},{256,320},{320,384},{3... | collective-permute-start | bytes 221192 | tf_op jit(solution)/shard_map/ppermute | solution.py:28
  49.2 26.5 %collective-permute-start.1 = (bf16[256,1536]{1,0:T(8,128)(2,1)S(1)}, bf16[256,1536]{1,0:T(8,128)(2,1)S(1)}, u32[]{:S(2)}, u32[]{:S(2)}) collective-permute-start(bf16[256,1536]{1,0:T(8,128)(2,1)S(1)} %bitcast.54), channel_id=1, source_target_pairs={{448,0},{0,64},{64,128},{128,192},{192,256},{256,320},{320,384},{3... | collective-permute-start | bytes 2359304 | tf_op jit(solution)/shard_map/ppermute | solution.py:28
  70.3 17.5 %all-to-all-start.2 = ((bf16[8,80,768]{2,1,0:T(8,128)(2,1)}), bf16[8,80,768]{2,1,0:T(8,128)(2,1)S(1)}, u32[]{:S(2)}, u32[]{:S(2)}) async-start(bf16[8,80,768]{2,1,0:T(8,128)(2,1)} %bitcast.43), calls=%async_computation.2 | async-start | bytes 1966080 | tf_op jit(solution)/shard_map/all_to_all | solution.py:161
  87.8 1.0 copy-start.1
Sparse Core Ops, SparseCore 0:
  22.0 85.1 all-gather.2

commit v6 on v5

--- a/solution.py
+++ b/solution.py
@@ -134,12 +134,6 @@
     ).reshape(Y * COLS, FW)
     slab, block_count, mod_table, hidden = lax.optimization_barrier((slab, block_count, mod_table, hidden))
     weight = lax.all_gather(slab, "frames", axis=0, tiled=True, axis_index_groups=Z_GROUPS)
-    stream_in = from_behind(hidden[0], "segment", 1)
-    levels = mod_table.shape[1]
-    onehot = (timestep[0][:, None] == jnp.arange(levels, dtype=jnp.int32)[None, :]).astype(jnp.float32)
-    modulate = jnp.sum(onehot[:, :, None, None] * mod_table[0][None], axis=1)
-    modulate = from_behind(modulate.reshape(12, DW), "segment", 1).reshape(4, 3, DW)
-
     counts = block_count[0]
     before = jnp.arange(4, dtype=jnp.int32)[:, None] > jnp.arange(4, dtype=jnp.int32)[None, :]
     start = jnp.sum(jnp.where(before, counts[None, :], 0), axis=1)
@@ -157,6 +151,13 @@
     part = lax.dynamic_slice(features, (me * PART, 0), (PART, FW))
     table = lax.all_to_all(jnp.broadcast_to(part[None], (Z, PART, FW)), "frames", 0, 0, axis_index_groups=Z_GROUPS)
     table = lax.all_gather(table.reshape(Z * PART, FW), "frames", axis=0, tiled=True, axis_index_groups=Y_GROUPS)
+    table, mod_table, hidden = lax.optimization_barrier((table, mod_table, hidden))
+    stream_in = from_behind(hidden[0], "segment", 1)
+    levels = mod_table.shape[1]
+    onehot = (timestep[0][:, None] == jnp.arange(levels, dtype=jnp.int32)[None, :]).astype(jnp.float32)
+    modulate = jnp.sum(onehot[:, :, None, None] * mod_table[0][None], axis=1)
+    modulate = from_behind(modulate.reshape(12, DW), "segment", 1).reshape(4, 3, DW)
+
     picked = pick(spot.reshape(-1), table.reshape(Z * Y, PART, FW))
     picked = lax.all_to_all(picked.reshape(SEG, LIVE * PART, FW), "segment", 0, 0)
     picked = picked.reshape(SEG, LIVE, PART, FW).transpose(1, 0, 2, 3).reshape(LIVE * BLK, FW)

time: 124 us -> 124 us (level)
    ppermute x3, waiting for transfers between devices: 5.37 us -> 24.2 us  [from_behind(): return lax.ppermute(block, axis, route)]
    all_to_all x1, waiting for transfers between devices: 11.4 us -> 0.01 us  [local(): lax.all_to_all(picked.reshape(SEG, LIVE * PART, FW), 'segment', 0, 0)]
    all_gather x1, waiting for transfers between devices: 17.2 us -> 6.44 us  [local(): lax.all_gather(slab, 'frames', axis=0, tiled=True, axis_index_groups=Z_GR...]
    all_to_all x1, waiting for transfers between devices: 0.6 us -> 4.94 us  [local(): lax.all_to_all(jnp.broadcast_to(part[None], (Z, PART, FW)), 'frames', 0,...]
    ppermute x3, starting transfers between devices: 1.9 us -> 0.18 us  [from_behind(): return lax.ppermute(block, axis, route)]
  transfers between devices with their start and end apart: 6 -> 6, of which waited for: 5 -> 4; matrix products, arithmetic and copies ran while one was open for 5% -> 5% of each run, Pallas kernels for 2% -> 2%
where the time goes in v6:
time: 124 us; the launch traced here: 123 us
  waiting for transfers between devices  35.6 us (29%)
  blocking collectives  33.5 us (27%)
  starting transfers between devices  21.6 us (17%)
  between operations  14.2 us (11%)
  Pallas kernels  11.4 us (9%)
  local copies, waits for them, and re-layouts  5.33 us (4%)
  other arithmetic  1.51 us (1%)
    ppermute x3, waiting for transfers between devices, from_behind(): return lax.ppermute(block, axis, route)  24.2 us
    all_to_all x1, starting transfers between devices, local(): lax.all_to_all(jnp.broadcast_to(part[None], (Z, PART, FW)), 'frames', 0,...  15.2 us
    all_gather x1, blocking collectives, local(): lax.all_gather(table.reshape(Z * PART, FW), 'frames', axis=0, tiled=True,...  14.7 us
    all_to_all x1, blocking collectives, local(): lax.all_to_all(jnp.broadcast_to(slab[None], (Y, COLS, FW)), 'frames', 0,...  11.2 us
    pallas_call x1, Pallas kernels, attention(): pl.pallas_call(attend, out_shape=jax.ShapeDtypeStruct((4 * BLK, DW), jnp....  9.09 us
    unnamed x1, blocking collectives  7.57 us
    all_gather x1, waiting for transfers between devices, local(): lax.all_gather(slab, 'frames', axis=0, tiled=True, axis_index_groups=Z_GR...  6.44 us
    all_to_all x1, starting transfers between devices, local(): lax.all_to_all(picked.reshape(SEG, LIVE * PART, FW), 'segment', 0, 0)  6.15 us
  transfers between devices with their start and end apart: 6, of which 4 were waited for; matrix products, arithmetic and copies ran while one was open for 5% of the time, Pallas kernels for 2%

profile of v6, /device:TPU:4, one launch (start us, length us, event | category | flops | bytes accessed | tf_op | source)
XLA Modules:
  0.0 123.1 jit_solution(16212937127982938365)
XLA Ops:
  6.5 0.0 all-gather.3.cloned.1.call-start
  6.6 4.0 %collective-permute-done = bf16[48,768]{1,0:T(8,128)(2,1)S(1)} collective-permute-done((bf16[48,768]{1,0:T(8,128)(2,1)}, bf16[48,768]{1,0:T(8,128)(2,1)S(1)}, u32[]{:S(2)}, u32[]{:S(2)}) %collective-permute-start) | collective-permute-done | bytes 73760 | tf_op jit(solution)/shard_map/ppermute | solution.py:28
  10.6 11.2 %all_to_all.15 = bf16[4,48,768]{2,1,0:T(8,128)(2,1)} all-to-all(bf16[4,48,768]{2,1,0:T(8,128)(2,1)S(1)} %broadcast_in_dim.54), channel_id=1, replica_groups={{0,16,32,48},{1,17,33,49},{2,18,34,50},{3,19,35,51},{4,20,36,52},{5,21,..., dimensions={0} | all-to-all | bytes 589824 | tf_op jit(solution)/shard_map/all_to_all | solution.py:132
  21.8 0.0 all-gather.3.cloned.1.call-update
  21.9 0.7 broadcast_in_dim.61
  22.6 15.2 %all-to-all-start.1 = ((bf16[16,8,768]{2,1,0:T(8,128)(2,1)}), bf16[16,8,768]{2,1,0:T(8,128)(2,1)S(1)}, u32[]{:S(2)}, u32[]{:S(2)}) async-start(bf16[16,8,768]{2,1,0:T(8,128)(2,1)} %broadcast_in_dim.61), calls=%async_computation.1 | async-start | bytes 393216 | tf_op jit(solution)/shard_map/all_to_all | solution.py:152
  37.8 1.3 %dynamic-slice = u32[1]{0:T(128)} dynamic-slice(u32[512]{0:T(512)} %constant.35, u32[]{:T(128)S(6)} %add.63), dynamic_slice_sizes={1} | dynamic-slice | bytes 12
  39.7 0.1 fusion.4
  39.8 0.1 select_reduce_fusion.1
  39.9 0.1 add_select_fusion
  40.0 0.1 select_reduce_fusion
  40.1 0.2 add_dynamic-update-slice_fusion
  40.3 7.6 %all-reduce = s32[144]{0:T(256)S(1)} all-reduce(s32[144]{0:T(256)S(1)} %add_dynamic-update-slice_fusion), channel_id=2, replica_groups=mesh['segment'=8,'frames'=64] {'segment'}, use_global_device_ids=true, to_apply=%add | all-reduce | flops 144 | bytes 1152
  47.9 0.1 reshape.126
  47.9 0.1 slice_bitcast_fusion
  48.0 0.1 constant_dynamic-slice_fusion
  48.1 0.1 slice_bitcast_fusion.1
  48.2 4.9 %all-to-all-done.1 = bf16[16,8,768]{2,1,0:T(8,128)(2,1)S(1)} async-done(((bf16[16,8,768]{2,1,0:T(8,128)(2,1)}), bf16[16,8,768]{2,1,0:T(8,128)(2,1)S(1)}, u32[]{:S(2)}, u32[]{:S(2)}) %all-to-all-start.1) | async-done | bytes 196640 | tf_op jit(solution)/shard_map/all_to_all | solution.py:152
  53.1 14.7 %all_gather.10 = bf16[512,768]{1,0:T(8,128)(2,1)} all-gather(bf16[128,768]{1,0:T(8,128)(2,1)S(1)} %bitcast.46), channel_id=1, replica_groups={{0,16,32,48},{1,17,33,49},{2,18,34,50},{3,19,35,51},{4,20,36,52},{5,21,..., dimensions={0}, use_global_device_ids=true | all-gather | bytes 983040 | tf_op jit(solution)/shard_map/all_gather | solution.py:153
  67.8 0.4 multiply_reduce_fusion
  68.3 0.6 reshape.115.spot
  68.9 2.3 %shard_map.73 = bf16[80,8,768]{2,1,0:T(8,128)(2,1)} custom-call(s32[80]{0:T(128)} %reshape.115.spot, bf16[64,8,768]{2,1,0:T(8,128)(2,1)} %bitcast.44), custom_call_target="tpu_custom_call" | custom-call | tf_op jit(solution)/shard_map/pallas_call | solution.py:121
  71.2 6.2 %all-to-all-start.2 = ((bf16[8,80,768]{2,1,0:T(8,128)(2,1)}), bf16[8,80,768]{2,1,0:T(8,128)(2,1)S(1)}, u32[]{:S(2)}, u32[]{:S(2)}) async-start(bf16[8,80,768]{2,1,0:T(8,128)(2,1)} %bitcast.43), calls=%async_computation.2 | async-start | bytes 1966080 | tf_op jit(solution)/shard_map/all_to_all | solution.py:162
  77.3 0.1 collective-permute-start.1
  77.5 0.1 fusion.5
  77.6 20.2 %collective-permute-done.1.hid_ref = bf16[256,1536]{1,0:T(8,128)(2,1)S(1)} collective-permute-done((bf16[256,1536]{1,0:T(8,128)(2,1)S(1)}, bf16[256,1536]{1,0:T(8,128)(2,1)S(1)}, u32[]{:S(2)}, u32[]{:S(2)}) %collective-permute-start.1) | collective-permute-done | bytes 786464 | tf_op jit(solution)/shard_map/ppermute | solution.py:28
  97.9 0.2 fusion
  98.1 0.3 fusion.3.q_ref
  98.4 1.0 copy-done.1
  99.4 1.3 %copy.12 = bf16[10,8,8,768]{3,2,1,0:T(8,128)(2,1)S(1)} copy(bf16[10,8,8,768]{3,2,0,1:T(8,128)(2,1)} %bitcast.42) | data formatting | bytes 1966080 | tf_op jit(solution)/shard_map/transpose | solution.py:163
  100.7 6.4 %all-gather.3.cloned.1.call-done = bf16[3072,768]{1,0:T(8,128)(2,1)} async-done(((bf16[192,768]{1,0:T(8,128)(2,1)}), bf16[3072,768]{1,0:T(8,128)(2,1)}) %all-gather.3.cloned.1.call-update) | async-done | bytes 4718608 | tf_op jit(solution)/shard_map/all_gather | solution.py:136
  107.2 9.1 %shard_map.74 = bf16[256,1536]{1,0:T(8,128)(2,1)} custom-call(s32[4]{0:T(128)S(1)} %broadcast_minimum_fusion.first, s32[4]{0:T(128)S(1)} %get-tuple-element.23.start, s32[4]{0:T(128)S(1)} %get-tuple-element.22.count, bf16[640,768]{1,0:T(8,128)(2,1)S(1)} %bitcast.39, bf16[256,1536]{1,0:T(8,128)(2,1)S(1)} %fusion.3.q_ref, ...), custom_call_target="tpu_custom_call" | custom-call | tf_op jit(solution)/shard_map/pallas_call | solution.py:97
  (28 shorter events, 0.2 us)
Async XLA Ops:
  6.5 15.3 %copy-start = (bf16[64,768]{1,0:T(8,128)(2,1)S(1)}, bf16[64,768]{1,0:T(8,128)(2,1)}, u32[]{:S(2)}) copy-start(bf16[64,768]{1,0:T(8,128)(2,1)} %param.8) | copy-start | bytes 294916
  6.5 33.3 %copy-start.4 = (s32[1,4]{1,0:T(1,128)S(1)}, s32[1,4]{1,0:T(1,128)}, u32[]{:S(2)}) copy-start(s32[1,4]{1,0:T(1,128)} %param.13) | copy-start | bytes 52
  6.5 61.3 %copy-start.2 = (f32[1,32,3,1536]{3,1,2,0:T(8,128)S(1)}, f32[1,32,3,1536]{3,1,2,0:T(8,128)}, u32[]{:S(2)}) copy-start(f32[1,32,3,1536]{3,1,2,0:T(8,128)} %param.10) | copy-start | bytes 1769476
  6.5 33.2 %copy-start.5 = (s32[1,4]{1,0:T(1,128)S(1)}, s32[1,4]{1,0:T(1,128)}, u32[]{:S(2)}) copy-start(s32[1,4]{1,0:T(1,128)} %param.11) | copy-start | bytes 52
  6.5 33.5 %copy-start.3 = (s32[1,4,4]{2,1,0:T(4,128)S(1)}, s32[1,4,4]{2,1,0:T(4,128)}, u32[]{:S(2)}) copy-start(s32[1,4,4]{2,1,0:T(4,128)} %param.12) | copy-start | bytes 196
  6.5 100.6 %all-gather.3.cloned.1.call-start = ((), (), s32[]{:S(2)}) async-start(), calls=%async_computation.3 | async-start | bytes 5013504 | tf_op jit(solution)/shard_map/all_gather | solution.py:136
  6.6 4.0 %collective-permute-start = (bf16[48,768]{1,0:T(8,128)(2,1)}, bf16[48,768]{1,0:T(8,128)(2,1)S(1)}, u32[]{:S(2)}, u32[]{:S(2)}) collective-permute-start(bf16[48,768]{1,0:T(8,128)(2,1)} %bitcast.55), channel_id=1, source_target_pairs={{448,0},{0,64},{64,128},{128,192},{192,256},{256,320},{320,384},{3... | collective-permute-start | bytes 221192 | tf_op jit(solution)/shard_map/ppermute | solution.py:28
  22.6 30.5 %all-to-all-start.1 = ((bf16[16,8,768]{2,1,0:T(8,128)(2,1)}), bf16[16,8,768]{2,1,0:T(8,128)(2,1)S(1)}, u32[]{:S(2)}, u32[]{:S(2)}) async-start(bf16[16,8,768]{2,1,0:T(8,128)(2,1)} %broadcast_in_dim.61), calls=%async_computation.1 | async-start | bytes 393216 | tf_op jit(solution)/shard_map/all_to_all | solution.py:152
  68.2 9.2 %collective-permute-start.2 = (f32[12,1536]{1,0:T(8,128)S(1)}, f32[12,1536]{1,0:T(8,128)S(1)}, u32[]{:S(2)}, u32[]{:S(2)}) collective-permute-start(f32[12,1536]{1,0:T(8,128)S(1)} %reshape.121), channel_id=1, source_target_pairs={{448,0},{0,64},{64,128},{128,192},{192,256},{256,320},{320,384},{3... | collective-permute-start | bytes 221192 | tf_op jit(solution)/shard_map/ppermute | solution.py:28
  68.9 8.5 %copy-start.6 = (bf16[1,256,1536]{2,1,0:T(8,128)(2,1)S(1)}, bf16[1,256,1536]{2,1,0:T(8,128)(2,1)}, u32[]{:S(2)}) copy-start(bf16[1,256,1536]{2,1,0:T(8,128)(2,1)} %param.7) | copy-start | bytes 2359300
  71.2 27.2 %all-to-all-start.2 = ((bf16[8,80,768]{2,1,0:T(8,128)(2,1)}), bf16[8,80,768]{2,1,0:T(8,128)(2,1)S(1)}, u32[]{:S(2)}, u32[]{:S(2)}) async-start(bf16[8,80,768]{2,1,0:T(8,128)(2,1)} %bitcast.43), calls=%async_computation.2 | async-start | bytes 1966080 | tf_op jit(solution)/shard_map/all_to_all | solution.py:162
  77.3 20.5 %collective-permute-start.1 = (bf16[256,1536]{1,0:T(8,128)(2,1)S(1)}, bf16[256,1536]{1,0:T(8,128)(2,1)S(1)}, u32[]{:S(2)}, u32[]{:S(2)}) collective-permute-start(bf16[256,1536]{1,0:T(8,128)(2,1)S(1)} %bitcast.54), channel_id=1, source_target_pairs={{448,0},{0,64},{64,128},{128,192},{192,256},{256,320},{320,384},{3... | collective-permute-start | bytes 2359304 | tf_op jit(solution)/shard_map/ppermute | solution.py:28
  98.4 1.0 copy-start.1
Sparse Core Ops, SparseCore 0:
  22.0 85.1 all-gather.2
